TPU v7x, 256 devices: a whole 4x4x8 slice. The times are simulated.
256 devices in a mesh: sec: 64 (over z, y, core), slab: 4 (over x).
Axes of the slice: x: 4, y: 4, z: 8, core: 2. Of those that a mesh axis runs over, the one named last changes fastest.
Arguments:
- basis: bfloat16 [128, 1024, 1024], P('sec'), may hold values from -0.1875 to 0.1875
- fermion: bfloat16 [3, 128, 1024, 1024], P(None, 'sec', None, 'slab'), may hold values from -6 to 6
- partner: int32 [3, 128], P(None, 'sec'), may hold values from 0 to 127, as said below
Outputs:
- rotated: bfloat16 [3, 128, 1024, 1024], P(None, 'sec', 'slab')
Inputs may be any that keep to these rules, and one draw needn't show every extreme that they name: partner[f, Q] // 2 equals Q // 2 or (Q // 2 + 1) % 64, so a partner lies in the block of 2 sectors that holds Q or in the next block, the last block's next being the first.
All inputs are finite; a program needn't handle non-finite values.
Results may differ from a plain program's by a relative error of at most 0.0049.
Values may be sent and summed in bfloat16 or wider, within the bound.
A program may use at most 64 MiB of HBM per device.

v0:
```python
import jax
import jax.numpy as jnp
from jax import lax
from jax.sharding import PartitionSpec as P


def shifted(block, axis, distance):
    devices = range(lax.axis_size(axis))
    route = [((i - distance) % len(devices), i) for i in devices]
    return lax.ppermute(block, axis, route)


def left_product(left_block, right_block):
    return lax.dot_general(
        left_block, right_block, (((0,), (0,)), ((), ())), preferred_element_type=jnp.float32
    ).astype(jnp.bfloat16)


def local(basis, fermion, partner):
    sectors_here = basis.shape[0]
    flavours = fermion.shape[0]
    all_sectors = sectors_here * lax.axis_size("sec")
    first_sector = lax.axis_index("sec") * sectors_here
    following = shifted(basis, "sec", -1)
    half_blocks = []
    for flavour in range(flavours):
        per_sector = []
        for sector in range(sectors_here):
            per_sector.append(left_product(basis[sector], fermion[flavour, sector]))
        half_blocks.append(jnp.stack(per_sector))
    half_rotated = jnp.stack(half_blocks)
    row_slabs = lax.all_to_all(half_rotated, "slab", split_axis=2, concat_axis=3, tiled=True)
    local_index = (partner - first_sector) % all_sectors
    out_blocks = []
    for flavour in range(flavours):
        per_sector = []
        for sector in range(sectors_here):
            where_index = local_index[flavour, sector]
            rows_here = row_slabs[flavour, sector]

            def from_own(operand):
                chosen = lax.dynamic_index_in_dim(
                    basis, jnp.minimum(where_index, sectors_here - 1), 0, keepdims=False
                )
                return jnp.dot(operand, chosen, preferred_element_type=jnp.float32)

            def from_next(operand):
                chosen = lax.dynamic_index_in_dim(
                    following, jnp.maximum(where_index - sectors_here, 0), 0, keepdims=False
                )
                return jnp.dot(operand, chosen, preferred_element_type=jnp.float32)

            product = lax.cond(where_index < sectors_here, from_own, from_next, rows_here)
            per_sector.append(product.astype(jnp.bfloat16))
        out_blocks.append(jnp.stack(per_sector))
    return jnp.stack(out_blocks)


def solution(mesh):
    placed = (P("sec", None, None), P(None, "sec", None, "slab"), P(None, "sec"))
    return jax.shard_map(
        local, mesh=mesh, in_specs=placed, out_specs=P(None, "sec", "slab", None), check_vma=False
    )
```

profile of v0, /device:TPU:249, one launch (start us, length us, event | category | flops | bytes accessed | tf_op | source)
XLA Modules:
  0.0 90.7 jit_solution(14583612871458534378)
XLA Ops:
  0.0 0.7 collective-permute-start
  0.7 2.8 %fusion.159 = bf16[1,1024,256]{2,1,0:T(8,128)(2,1)S(1)} fusion(bf16[2,1024,1024]{2,1,0:T(8,128)(2,1)} %param.15, bf16[3,2,1024,256]{3,2,1,0:T(8,128)(2,1)} %param.16), kind=kOutput, calls=%fused_computation.99 | convolution fusion | flops 537133056 | bytes 3145728 | tf_op jit(solution)/shard_map/dot_general | solution.py:14
  3.5 0.5 copy-done.6
  4.0 0.8 fusion.156
  4.7 0.8 fusion.165
  5.6 0.8 fusion.162
  6.4 0.8 fusion.168
  7.2 0.8 fusion.171
  8.2 0.3 pad_maximum_fusion
  8.5 4.9 %copy.11 = bf16[3,2,1024,256]{3,1,0,2:T(2,128)(2,1)} copy(bf16[3,2,1024,256]{3,2,1,0:T(8,128)(2,1)S(1)} %pad_maximum_fusion) | data formatting | bytes 6291456 | tf_op jit(solution)/shard_map/stack | solution.py:31
  13.4 4.1 %all-to-all-start = ((bf16[3,2,1024,256]{3,1,0,2:T(2,128)(2,1)}), bf16[3,2,1024,256]{3,1,0,2:T(2,128)(2,1)S(1)}, u32[]{:S(2)}, u32[]{:S(2)}) async-start(bf16[3,2,1024,256]{3,1,0,2:T(2,128)(2,1)} %copy.11), calls=%async_computation | async-start | bytes 6291456 | tf_op jit(solution)/shard_map/all_to_all | solution.py:32
  17.6 0.7 fusion.187
  22.0 32.3 %all-to-all-done = bf16[3,2,1024,256]{3,1,0,2:T(2,128)(2,1)S(1)} async-done(((bf16[3,2,1024,256]{3,1,0,2:T(2,128)(2,1)}), bf16[3,2,1024,256]{3,1,0,2:T(2,128)(2,1)S(1)}, u32[]{:S(2)}, u32[]{:S(2)}) %all-to-all-start) | async-done | bytes 3145760 | tf_op jit(solution)/shard_map/all_to_all | solution.py:32
  54.3 4.1 %copy.12 = bf16[3,2,256,4,256]{4,3,2,1,0:T(4,128)(2,1)} copy(bf16[3,2,256,4,256]{4,1,0,2,3:T(2,128)(2,1)S(1)} %bitcast.245) | data formatting | bytes 6291456 | tf_op jit(solution)/shard_map/all_to_all | solution.py:32
  58.4 4.7 %all_to_all.16 = bf16[3,2,256,1024]{3,2,1,0:T(8,128)(2,1)S(1)} reshape(bf16[3,2,256,4,256]{4,3,2,1,0:T(4,128)(2,1)} %copy.12) | data formatting | bytes 6291456 | tf_op jit(solution)/shard_map/all_to_all | solution.py:32
  63.1 1.7 %slice_bitcast_fusion.5 = (bf16[256,1024]{1,0:T(8,128)(2,1)}, bf16[256,1024]{1,0:T(8,128)(2,1)}, bf16[256,1024]{1,0:T(8,128)(2,1)}, bf16[256,1024]{1,0:T(8,128)(...) fusion(bf16[3,2,256,1024]{3,2,1,0:T(8,128)(2,1)S(1)} %all_to_all.16), kind=kLoop, calls=%fused_computation.115 | loop fusion | bytes 6291456 | tf_op jit(solution)/shard_map/squeeze | solution.py:39
  64.8 3.3 %conditional.6 = (bf16[1,256,1024]{2,1,0:T(8,128)(2,1)S(1)}) conditional(s32[]{:T(128)} %convert_element_type.114, (s32[]{:T(128)}, bf16[2,1024,1024]{2,1,0:T(8,128)(2,1)}, bf16[256,1024]{1,0:T(8,128)(2,1)}) %tuple.53, (s32[]{:T(128)}, bf16[2,1024,1024]{2,1,0:T(8,128)(2,1)}, bf16[256,1024]{1,0:T(8,128)(2,1)}) %tuple.54), branch_computations={%region_0.1_spmd, %region_1.2_spmd} | conditional | flops 537133056 | bytes 4194362 | solution.py:53
  65.5 2.4 %fusion.16 = bf16[1,256,1024]{1,2,0:T(8,128)(2,1)S(1)} fusion(bf16[256,1024]{1,0:T(8,128)(2,1)} %get-tuple-element.106, bf16[2,1024,1024]{2,1,0:T(8,128)(2,1)} %get-tuple-element.104, s32[]{:T(128)S(6)} %select_n.25), kind=kOutput, calls=%fused_computation.10 | convolution fusion | flops 537133056 | bytes 3145732 | tf_op jit(solution)/shard_map/cond/branch_1_fun/dot_general | solution.py:45
  67.9 0.2 copy.20
  68.2 3.3 %conditional.7 = (bf16[1,256,1024]{2,1,0:T(8,128)(2,1)S(1)}) conditional(s32[]{:T(128)} %convert_element_type.121, (s32[]{:T(128)}, bf16[2,1024,1024]{2,1,0:T(8,128)(2,1)}, bf16[256,1024]{1,0:T(8,128)(2,1)S(1)}) %tuple.106, (s32[]{:T(128)}, bf16[2,1024,1024]{2,1,0:T(8,128)(2,1)}, bf16[256,1024]{1,0:T(8,128)(2,1)S(1)}) %tuple.107), branch_computations={%region_2.3_spmd, %region_3.4_spmd} | conditional | flops 537133056 | bytes 4194362 | solution.py:53
  68.9 2.4 %fusion.26 = bf16[1,256,1024]{1,2,0:T(8,128)(2,1)S(1)} fusion(bf16[256,1024]{1,0:T(8,128)(2,1)S(1)} %get-tuple-element.109, bf16[2,1024,1024]{2,1,0:T(8,128)(2,1)} %get-tuple-element.107, s32[]{:T(128)S(6)} %max.13), kind=kOutput, calls=%fused_computation.16 | convolution fusion | flops 537133056 | bytes 3145732 | tf_op jit(solution)/shard_map/cond/branch_0_fun/dot_general | solution.py:51
  71.6 3.3 %conditional.8 = (bf16[1,256,1024]{2,1,0:T(8,128)(2,1)S(1)}) conditional(s32[]{:T(128)} %convert_element_type.122, (s32[]{:T(128)}, bf16[2,1024,1024]{2,1,0:T(8,128)(2,1)}, bf16[256,1024]{1,0:T(8,128)(2,1)S(1)}) %tuple.104, (s32[]{:T(128)}, bf16[2,1024,1024]{2,1,0:T(8,128)(2,1)}, bf16[256,1024]{1,0:T(8,128)(2,1)S(1)}) %tuple.105), branch_computations={%region_4.5_spmd, %region_5.6_spmd} | conditional | flops 537133056 | bytes 4194362 | solution.py:53
  72.3 2.4 %fusion.56 = bf16[1,256,1024]{1,2,0:T(8,128)(2,1)S(1)} fusion(bf16[256,1024]{1,0:T(8,128)(2,1)S(1)} %get-tuple-element.118, bf16[2,1024,1024]{2,1,0:T(8,128)(2,1)} %get-tuple-element.116, s32[]{:T(128)S(6)} %select_n.27), kind=kOutput, calls=%fused_computation.34 | convolution fusion | flops 537133056 | bytes 3145732 | tf_op jit(solution)/shard_map/cond/branch_1_fun/dot_general | solution.py:45
  74.9 3.2 %conditional.9 = (bf16[1,256,1024]{2,1,0:T(8,128)(2,1)S(1)}) conditional(s32[]{:T(128)} %convert_element_type.123, (s32[]{:T(128)}, bf16[2,1024,1024]{2,1,0:T(8,128)(2,1)}, bf16[256,1024]{1,0:T(8,128)(2,1)S(1)}) %tuple.102, (s32[]{:T(128)}, bf16[2,1024,1024]{2,1,0:T(8,128)(2,1)}, bf16[256,1024]{1,0:T(8,128)(2,1)S(1)}) %tuple.103), branch_computations={%region_6.7_spmd, %region_7.8_spmd} | conditional | flops 537133056 | bytes 4194362 | solution.py:53
  75.5 2.4 %fusion.66 = bf16[1,256,1024]{1,2,0:T(8,128)(2,1)S(1)} fusion(bf16[256,1024]{1,0:T(8,128)(2,1)S(1)} %get-tuple-element.121, bf16[2,1024,1024]{2,1,0:T(8,128)(2,1)} %get-tuple-element.119, s32[]{:T(128)S(6)} %max.15), kind=kOutput, calls=%fused_computation.40 | convolution fusion | flops 537133056 | bytes 3145732 | tf_op jit(solution)/shard_map/cond/branch_0_fun/dot_general | solution.py:51
  78.2 5.4 %conditional.10 = (bf16[1,256,1024]{2,1,0:T(8,128)(2,1)S(1)}) conditional(s32[]{:T(128)} %convert_element_type.124, (s32[]{:T(128)}, bf16[2,1024,1024]{2,1,0:T(8,128)(2,1)}, bf16[256,1024]{1,0:T(8,128)(2,1)}) %tuple.61, (s32[]{:T(128)}, bf16[2,1024,1024]{2,1,0:T(8,128)(2,1)}, bf16[256,1024]{1,0:T(8,128)(2,1)}) %tuple.62), branch_computations={%region_8.9_spmd, %region_9.10_spmd} | conditional | flops 537133056 | bytes 4194362 | solution.py:53
  79.1 3.2 %fusion.96 = bf16[1,256,1024]{1,2,0:T(8,128)(2,1)} fusion(bf16[256,1024]{1,0:T(8,128)(2,1)} %get-tuple-element.130, bf16[2,1024,1024]{2,1,0:T(8,128)(2,1)} %get-tuple-element.128, s32[]{:T(128)S(6)} %select_n.29), kind=kOutput, calls=%fused_computation.58 | convolution fusion | flops 537133056 | bytes 3145732 | tf_op jit(solution)/shard_map/cond/branch_1_fun/dot_general | solution.py:45
  82.4 1.2 %copy.28 = bf16[1,256,1024]{2,1,0:T(8,128)(2,1)S(1)} copy(bf16[1,256,1024]{1,2,0:T(8,128)(2,1)} %fusion.96) | data formatting | bytes 1048576 | tf_op jit(solution)/shard_map/cond | solution.py:53
  83.6 5.0 %conditional.11 = (bf16[1,256,1024]{2,1,0:T(8,128)(2,1)S(1)}) conditional(s32[]{:T(128)} %convert_element_type.125, (s32[]{:T(128)}, bf16[2,1024,1024]{2,1,0:T(8,128)(2,1)}, bf16[256,1024]{1,0:T(8,128)(2,1)S(1)}) %tuple.100, (s32[]{:T(128)}, bf16[2,1024,1024]{2,1,0:T(8,128)(2,1)}, bf16[256,1024]{1,0:T(8,128)(2,1)S(1)}) %tuple.101), branch_computations={%region_10.11_spmd, %region_11.12_spmd} | conditional | flops 537133056 | bytes 4194362 | solution.py:53
  84.2 3.2 %fusion.106 = bf16[1,256,1024]{1,2,0:T(8,128)(2,1)} fusion(bf16[256,1024]{1,0:T(8,128)(2,1)S(1)} %get-tuple-element.133, bf16[2,1024,1024]{2,1,0:T(8,128)(2,1)} %get-tuple-element.131, s32[]{:T(128)S(6)} %max.17), kind=kOutput, calls=%fused_computation.64 | convolution fusion | flops 537133056 | bytes 3145732 | tf_op jit(solution)/shard_map/cond/branch_0_fun/dot_general | solution.py:51
  87.3 1.2 %copy.29 = bf16[1,256,1024]{2,1,0:T(8,128)(2,1)S(1)} copy(bf16[1,256,1024]{1,2,0:T(8,128)(2,1)} %fusion.106) | data formatting | bytes 1048576 | tf_op jit(solution)/shard_map/cond | solution.py:53
  88.7 2.0 %pad_maximum_fusion.1 = bf16[3,2,256,1024]{3,2,1,0:T(8,128)(2,1)} fusion(bf16[1,2,256,1024]{3,2,1,0:T(8,128)(2,1)S(1)} %maximum_bitcast_fusion.5, bf16[1,2,256,1024]{3,2,1,0:T(8,128)(2,1)S(1)} %maximum_bitcast_fusion.4, bf16[1,2,256,1024]{3,2,1,0:T(8,128)(2,1)S(1)} %maximum_bitcast_fusion.3), kind=kLoop, calls=%fused_computation.73 | loop fusion | flops 3145728 | bytes 6291456 | tf_op jit(solution)/shard_map/stack | solution.py:56
  (23 shorter events, 1.2 us)
Async XLA Ops:
  0.0 3.4 %copy-start.5 = (bf16[2,1024,1024]{2,1,0:T(8,128)(2,1)S(1)}, bf16[2,1024,1024]{2,1,0:T(8,128)(2,1)}, u32[]{:S(2)}) copy-start(bf16[2,1024,1024]{2,1,0:T(8,128)(2,1)} %param.15) | copy-start | bytes 12582916
  0.0 4.0 %copy-start.6 = (bf16[3,2,1024,256]{3,2,1,0:T(8,128)(2,1)S(1)}, bf16[3,2,1024,256]{3,2,1,0:T(8,128)(2,1)}, u32[]{:S(2)}) copy-start(bf16[3,2,1024,256]{3,2,1,0:T(8,128)(2,1)} %param.16) | copy-start | bytes 9437188
  0.0 64.8 %collective-permute-start = (bf16[2,1024,1024]{2,1,0:T(8,128)(2,1)}, bf16[2,1024,1024]{2,1,0:T(8,128)(2,1)}, u32[]{:S(2)}, u32[]{:S(2)}) collective-permute-start(bf16[2,1024,1024]{2,1,0:T(8,128)(2,1)} %param.15), channel_id=1, source_target_pairs={{4,0},{8,4},{12,8},{16,12},{20,16},{24,20},{28,24},{32,28},{36,32}... | collective-permute-start | bytes 12582920 | tf_op jit(solution)/shard_map/ppermute | solution.py:10
  13.4 4.1 %copy-start.4 = (s32[3,2]{0,1:T(2,128)S(1)}, s32[3,2]{0,1:T(2,128)}, u32[]{:S(2)}) copy-start(s32[3,2]{0,1:T(2,128)} %param.17) | copy-start | bytes 76
  13.4 40.9 %all-to-all-start = ((bf16[3,2,1024,256]{3,1,0,2:T(2,128)(2,1)}), bf16[3,2,1024,256]{3,1,0,2:T(2,128)(2,1)S(1)}, u32[]{:S(2)}, u32[]{:S(2)}) async-start(bf16[3,2,1024,256]{3,1,0,2:T(2,128)(2,1)} %copy.11), calls=%async_computation | async-start | bytes 6291456 | tf_op jit(solution)/shard_map/all_to_all | solution.py:32
  64.8 3.4 %copy-start.3 = (bf16[256,1024]{1,0:T(8,128)(2,1)S(1)}, bf16[256,1024]{1,0:T(8,128)(2,1)}, u32[]{:S(2)}) copy-start(bf16[256,1024]{1,0:T(8,128)(2,1)} %get-tuple-element.148) | copy-start | bytes 1572868
  68.1 3.4 %copy-start.2 = (bf16[256,1024]{1,0:T(8,128)(2,1)S(1)}, bf16[256,1024]{1,0:T(8,128)(2,1)}, u32[]{:S(2)}) copy-start(bf16[256,1024]{1,0:T(8,128)(2,1)} %get-tuple-element.147) | copy-start | bytes 1572868
  71.6 3.3 %copy-start.1 = (bf16[256,1024]{1,0:T(8,128)(2,1)S(1)}, bf16[256,1024]{1,0:T(8,128)(2,1)}, u32[]{:S(2)}) copy-start(bf16[256,1024]{1,0:T(8,128)(2,1)} %get-tuple-element.146) | copy-start | bytes 1572868
  78.2 5.4 %copy-start = (bf16[256,1024]{1,0:T(8,128)(2,1)S(1)}, bf16[256,1024]{1,0:T(8,128)(2,1)}, u32[]{:S(2)}) copy-start(bf16[256,1024]{1,0:T(8,128)(2,1)} %get-tuple-element.144) | copy-start | bytes 1572868
where the time goes:
time: 92.5 us; the launch traced here: 90.7 us
  waiting for transfers between devices  32.3 us (35%)
  matrix products  22.5 us (24%)
  local copies, waits for them, and re-layouts  19.9 us (22%)
  starting transfers between devices  4.82 us (5%)
  loops' own time  4.29 us (5%)
  between operations  3.96 us (4%)
  other arithmetic  2.94 us (3%)
    all_to_all x1, waiting for transfers between devices, local(): lax.all_to_all(half_rotated, 'slab', split_axis=2, concat_axis=3, tiled=T...  32.3 us
    all_to_all x2, local copies, waits for them, and re-layouts, local(): lax.all_to_all(half_rotated, 'slab', split_axis=2, concat_axis=3, tiled=T...  8.77 us
    dot_general x3, matrix products, from_own(): return jnp.dot(operand, chosen, preferred_element_type=jnp.float32)  8.02 us
    dot_general x3, matrix products, from_next(): return jnp.dot(operand, chosen, preferred_element_type=jnp.float32)  7.86 us
    dot_general x6, matrix products, left_product(): lax.dot_general(left_block, right_block, (((0,), (0,)), ((), ())), prefer...  6.67 us
    another operation x1, local copies, waits for them, and re-layouts, local(): half_rotated = jnp.stack(half_blocks)  4.9 us
    another operation x6, loops' own time, local(): lax.cond(where_index < sectors_here, from_own, from_next, rows_here)  4.29 us
    all_to_all x1, starting transfers between devices, local(): lax.all_to_all(half_rotated, 'slab', split_axis=2, concat_axis=3, tiled=T...  4.14 us
  transfers between devices with their start and end apart: 2, of which 1 were waited for; matrix products, arithmetic and copies ran while one was open for 21% of the time, Pallas kernels for 0%

commit v1 on v0

v1 whole, which is shorter than its diff:
```python
import functools

import jax
import jax.numpy as jnp
from jax import lax
from jax.experimental import pallas as pl
from jax.experimental.pallas import tpu as pltpu
from jax.sharding import PartitionSpec as P

MESH = pl.DeviceIdType.MESH
NB = 1024
W = 256
NS = 4
FL = 3
SD = 2
B = FL * SD
SECS = 64
NY = 4
LP = 4


def kernel(
    basis, fermion, partner, out,
    uo, u0, u1, u2, u3, fer, half, hr, rbuf, yb1, yb2,
    lu, lf, lo, d_s, d_r, r1_s, r1_r, r2_s, r2_r, y_s, y_r, l1_s, l1_r, l2_s, l2_r, l3_s, l3_r,
):
    us = (u0, u1, u2, u3)
    sec = lax.axis_index("sec")
    me = lax.axis_index("slab")
    core = lax.rem(sec, 2)
    chip = sec // 2
    y = lax.rem(chip, NY)
    z = chip // NY
    nz = SECS // (2 * NY)
    xp, xm = lax.rem(me + 1, NS), lax.rem(me + 3, NS)
    xo = lax.rem(me + 2, NS)
    right, left = (sec, xp), (sec, xm)
    before = (lax.rem(sec + SECS - 1, SECS), me)
    after = (lax.rem(sec + 1, SECS), me)
    y_up, y_dn = lax.rem(y + 1, NY), lax.rem(y + NY - 1, NY)
    z_first = lax.rem(z + nz - jnp.where(y == 0, 1, 0), nz)
    hop1_to = ((z_first * NY + y_up) * 2, me)
    z_from = lax.rem(z + jnp.where(y == 1, 1, 0), nz)
    hop1_from = ((z_from * NY + y_dn) * 2, me)
    hop2_to = ((z * NY + y_up) * 2, me)
    hop2_from = ((z * NY + y_dn) * 2, me)
    hop3_to = ((z * NY + y_up) * 2 + 1, me)
    hop3_from = ((z * NY + y_dn) * 2, me)
    first_sector = sec * SD

    barrier = pltpu.get_barrier_semaphore()

    def greet(device):
        pl.semaphore_signal(barrier, inc=1, device_id=device, device_id_type=MESH)

    for device in (right, left, before, after):
        greet(device)

    @pl.when(core == 0)
    def _():
        for device in (hop1_to, hop1_from, hop2_to, hop2_from, hop3_to):
            greet(device)

    @pl.when(core == 1)
    def _():
        greet(hop3_from)

    def load_uo(j, q):
        return pltpu.make_async_copy(
            basis.at[q, :, pl.ds(pl.multiple_of(j * W, W), W)], uo.at[j, q], lu.at[j, q]
        )

    def load_f(b, f, q):
        return pltpu.make_async_copy(fermion.at[f, q], fer.at[b], lf.at[b])

    def load_u(j):
        return pltpu.make_async_copy(
            basis.at[:, :, pl.ds(j * W, W)], us[j].at[pl.ds(0, SD)], lo.at[j]
        )

    load_f(0, 0, 0).start()
    for j in (xo, xp, xm, me):
        load_uo(j, 0).start()
    for f in range(1, FL):
        load_f(f, f, 0).start()
    for j in range(NS):
        load_uo(j, 1).start()
    for f in range(FL):
        load_f(FL + f, f, 1).start()
    for j in range(NS):
        load_u(j).start()

    @pl.when(core == 0)
    def _():
        pl.semaphore_wait(barrier, 9)

    @pl.when(core == 1)
    def _():
        pl.semaphore_wait(barrier, 5)

    def follow(j):
        return pltpu.make_async_remote_copy(
            src_ref=uo.at[j], dst_ref=us[j].at[pl.ds(SD, SD)],
            send_sem=y_s.at[j], recv_sem=y_r.at[j], device_id=before, device_id_type=MESH,
        )

    def piece(ref, i):
        return ref.at[i // 2, pl.ds((i % 2) * (NB // 2), NB // 2)]

    def last_piece(i):
        return u3.at[SD + i // 2, pl.ds((i % 2) * (NB // 2), NB // 2)]

    def hop1(i):
        return pltpu.make_async_remote_copy(
            src_ref=piece(uo.at[NS - 1], i), dst_ref=yb1.at[i],
            send_sem=l1_s.at[i], recv_sem=l1_r.at[i], device_id=hop1_to, device_id_type=MESH,
        )

    def hop2(i):
        return pltpu.make_async_remote_copy(
            src_ref=yb1.at[i], dst_ref=yb2.at[i],
            send_sem=l2_s.at[i], recv_sem=l2_r.at[i], device_id=hop2_to, device_id_type=MESH,
        )

    def hop3(i):
        return pltpu.make_async_remote_copy(
            src_ref=yb2.at[i], dst_ref=last_piece(i),
            send_sem=l3_s.at[i], recv_sem=l3_r.at[i], device_id=hop3_to, device_id_type=MESH,
        )

    for q in range(SD):
        for j in range(NS):
            load_uo(j, q).wait()
    for j in range(NS - 1):
        follow(j).start()

    @pl.when(core == 1)
    def _():
        follow(NS - 1).start()

    @pl.when(core == 0)
    def _():
        for i in range(LP):
            hop1(i).start()

    H = W // 2

    def direct(b, k):
        return pltpu.make_async_remote_copy(
            src_ref=half.at[b, (xp, xm)[k]], dst_ref=hr.at[b, me],
            send_sem=d_s.at[b, k], recv_sem=d_r.at[b, k],
            device_id=(right, left)[k], device_id_type=MESH,
        )

    def relay1(b, k):
        return pltpu.make_async_remote_copy(
            src_ref=half.at[b, xo, pl.ds(k * H, H)], dst_ref=rbuf.at[b, k],
            send_sem=r1_s.at[b, k], recv_sem=r1_r.at[b, k],
            device_id=(right, left)[k], device_id_type=MESH,
        )

    def relay2(b, k):
        return pltpu.make_async_remote_copy(
            src_ref=rbuf.at[b, k], dst_ref=hr.at[b, (xm, xp)[k], pl.ds(k * H, H)],
            send_sem=r2_s.at[b, k], recv_sem=r2_r.at[b, k],
            device_id=(right, left)[k], device_id_type=MESH,
        )

    def first_product(b, q, d):
        return lax.dot_general(
            uo[d, q], fer[b], (((0,), (0,)), ((), ())), preferred_element_type=jnp.float32
        ).astype(jnp.bfloat16)

    def stage1(b, _):
        q = b // FL
        load_f(b, 0, 0).wait()
        half[b, xo] = first_product(b, q, xo)
        half[b, xp] = first_product(b, q, xp)
        relay1(b, 0).start()
        relay1(b, 1).start()
        half[b, xm] = first_product(b, q, xm)
        direct(b, 0).start()
        hr[b, me] = first_product(b, q, me)
        direct(b, 1).start()
        return 0

    lax.fori_loop(0, B, stage1, 0)

    def forward_x(b):
        for k in range(2):
            relay1(b, k).wait_recv()
            relay2(b, k).start()

    def forward_y1(i):
        @pl.when(core == 0)
        def _():
            hop1(i).wait_recv()
            hop2(i).start()

    def forward_y2(i):
        @pl.when(core == 0)
        def _():
            hop2(i).wait_recv()
            hop3(i).start()

    forward_y1(0)
    forward_y1(1)
    forward_x(0)
    forward_x(1)
    forward_y1(2)
    forward_y1(3)
    forward_x(2)
    forward_y2(0)
    forward_x(3)
    forward_y2(1)
    forward_y2(2)
    forward_x(4)
    forward_y2(3)
    forward_x(5)

    for j in range(NS):
        load_u(j).wait()

    def second_product(b, f, q, j):
        index = lax.rem(partner[f, q] - first_sector + SECS * SD, 2 * SD)
        rows = jnp.concatenate([hr[b, s] for s in range(NS)], axis=1)
        value = jnp.dot(rows, us[j][index], preferred_element_type=jnp.float32)
        out[f, q, :, j * W:(j + 1) * W] = value.astype(jnp.bfloat16)

    follow(0).wait_recv()
    follow(1).wait_recv()

    def early(b, _):
        for k in range(2):
            direct(b, k).wait_recv()
            relay2(b, k).wait_recv()
        q = b // FL
        f = b - q * FL
        second_product(b, f, q, 0)
        second_product(b, f, q, 1)
        return 0

    lax.fori_loop(0, B, early, 0)
    follow(2).wait_recv()

    @pl.when(core == 0)
    def _():
        follow(3).wait_recv()

    @pl.when(core == 1)
    def _():
        for i in range(LP):
            hop3(i).wait_recv()

    def late(b, _):
        q = b // FL
        f = b - q * FL
        second_product(b, f, q, 2)
        second_product(b, f, q, 3)
        return 0

    lax.fori_loop(0, B, late, 0)

    def drain(b, _):
        for k in range(2):
            direct(b, k).wait_send()
            relay1(b, k).wait_send()
            relay2(b, k).wait_send()
        return 0

    lax.fori_loop(0, B, drain, 0)
    for j in range(NS - 1):
        follow(j).wait_send()

    @pl.when(core == 1)
    def _():
        follow(NS - 1).wait_send()

    @pl.when(core == 0)
    def _():
        for i in range(LP):
            hop1(i).wait_send()
            hop2(i).wait_send()
            hop3(i).wait_send()


def local(basis, fermion, partner):
    bf16 = jnp.bfloat16
    dma = pltpu.SemaphoreType.DMA
    return pl.pallas_call(
        kernel,
        out_shape=jax.ShapeDtypeStruct((FL, SD, W, NB), bf16),
        in_specs=[
            pl.BlockSpec(memory_space=pl.ANY),
            pl.BlockSpec(memory_space=pl.ANY),
            pl.BlockSpec(memory_space=pltpu.SMEM),
        ],
        out_specs=pl.BlockSpec(memory_space=pltpu.VMEM),
        scratch_shapes=[
            pltpu.VMEM((NS, SD, NB, W), bf16),
            *[pltpu.VMEM((2 * SD, NB, W), bf16) for _ in range(NS)],
            pltpu.VMEM((B, NB, W), bf16),
            pltpu.VMEM((B, NS, W, W), bf16),
            pltpu.VMEM((B, NS, W, W), bf16),
            pltpu.VMEM((B, 2, W // 2, W), bf16),
            pltpu.VMEM((LP, NB // 2, W), bf16),
            pltpu.VMEM((LP, NB // 2, W), bf16),
            dma((NS, SD)), dma((B,)), dma((NS,)),
            *[dma((B, 2)) for _ in range(6)],
            dma((NS,)), dma((NS,)),
            *[dma((LP,)) for _ in range(6)],
        ],
        compiler_params=pltpu.CompilerParams(
            collective_id=0, has_side_effects=True, vmem_limit_bytes=60 * 2**20
        ),
    )(basis, fermion, partner)


def solution(mesh):
    placed = (P("sec", None, None), P(None, "sec", None, "slab"), P(None, "sec"))
    return jax.shard_map(
        local, mesh=mesh, in_specs=placed, out_specs=P(None, "sec", "slab", None), check_vma=False
    )
```

time: 92.5 us -> 81.4 us (0.88)
  the two profiles are of different devices: /device:TPU:249 before, /device:TPU:115 now
where the time goes in v1:
time: 81.4 us; the launch traced here: 81.3 us
  Pallas kernels  75.8 us (93%)
  local copies, waits for them, and re-layouts  5.47 us (7%)
    pallas_call x1, Pallas kernels, local(): pl.pallas_call(kernel, out_shape=jax.ShapeDtypeStruct((FL, SD, W, NB), bf...  75.8 us
    unnamed x2, local copies, waits for them, and re-layouts  5.47 us

profile of v1, /device:TPU:115, one launch (start us, length us, event | category | flops | bytes accessed | tf_op | source)
XLA Modules:
  0.0 81.3 jit_solution(15955393348409472163)
XLA Ops:
  0.0 1.3 %copy.4.partner = s32[3,2]{1,0:T(4,128)} copy(s32[3,2]{0,1:T(2,128)} %param.5) | data formatting | bytes 48 | tf_op args[2]
  1.3 75.8 %shard_map.37 = bf16[3,2,256,1024]{3,2,1,0:T(8,128)(2,1)} custom-call(bf16[2,1024,1024]{2,1,0:T(8,128)(2,1)} %basis.1, bf16[3,2,1024,256]{3,2,1,0:T(8,128)(2,1)} %fermion.1, s32[3,2]{1,0:T(4,128)} %copy.4.partner), custom_call_target="tpu_custom_call" | custom-call | tf_op jit(solution)/shard_map/pallas_call | solution.py:290
  77.1 4.1 %copy.6 = bf16[3,2,256,1024]{3,2,1,0:T(8,128)(2,1)} copy(bf16[3,2,256,1024]{3,2,1,0:T(8,128)(2,1)} %shard_map.37) | data formatting | bytes 6291456

commit v2 on v1

v2 whole, which is shorter than its diff:
```python
import functools

import jax
import jax.numpy as jnp
from jax import lax
from jax.experimental import pallas as pl
from jax.experimental.pallas import tpu as pltpu
from jax.sharding import PartitionSpec as P

MESH = pl.DeviceIdType.MESH
NB = 1024
W = 256
NS = 4
FL = 3
SD = 2
B = FL * SD
SECS = 64
NY = 4
LP = 4
KB = NB // LP
KA = NB - KB


def kernel(
    basis, fermion, partner, out,
    uo, u0, u1, u2a, u2b, u3a, u3b, fer, half, hr, rbuf, yb1, yb2, yb3, acc,
    lu, lf, lo, x_s, x_r, r1_r, y_s, y_r, l1_r, l2_r, l3_r, t_s, t_r,
):
    sec = lax.axis_index("sec")
    me = lax.axis_index("slab")
    core = lax.rem(sec, 2)
    chip = sec // 2
    y = lax.rem(chip, NY)
    z = chip // NY
    nz = SECS // (2 * NY)
    xp, xm = lax.rem(me + 1, NS), lax.rem(me + 3, NS)
    xo = lax.rem(me + 2, NS)
    right, left = (sec, xp), (sec, xm)
    before = (lax.rem(sec + SECS - 1, SECS), me)
    after = (lax.rem(sec + 1, SECS), me)
    y_up, y_dn = lax.rem(y + 1, NY), lax.rem(y + NY - 1, NY)
    hop_to = ((z * NY + y_up) * 2, me)
    hop_from = ((z * NY + y_dn) * 2, me)
    row_dn, row_up = lax.rem(z + nz - 1, nz), lax.rem(z + 1, nz)
    row_to = ((row_dn * NY + y) * 2, me)
    row_from = ((row_up * NY + y) * 2, me)
    end_to = ((z * NY + y_up) * 2 + 1, me)
    end_from = ((z * NY + y_dn) * 2, me)
    turns = y == 2
    first_sector = sec * SD

    barrier = pltpu.get_barrier_semaphore()

    def greet(device):
        pl.semaphore_signal(barrier, inc=1, device_id=device, device_id_type=MESH)

    for device in (right, left, before, after):
        greet(device)

    @pl.when(core == 0)
    def _():
        for device in (hop_to, hop_from, end_to):
            greet(device)

        @pl.when(turns)
        def _():
            greet(row_to)
            greet(row_from)

    @pl.when(core == 1)
    def _():
        greet(end_from)

    def load_uo(j, q):
        return pltpu.make_async_copy(
            basis.at[q, :, pl.ds(pl.multiple_of(j * W, W), W)], uo.at[j, q], lu.at[j, q]
        )

    def load_f(b, f, q):
        return pltpu.make_async_copy(fermion.at[f, q], fer.at[b], lf.at[b])

    def load_u(ref, j, row, rows, n):
        return pltpu.make_async_copy(
            basis.at[:, pl.ds(row, rows), pl.ds(j * W, W)], ref.at[pl.ds(0, SD)], lo.at[n]
        )

    def own_u():
        places = ((u0, 0, 0, NB), (u1, 1, 0, NB), (u2a, 2, 0, KA), (u2b, 2, KA, KB),
                  (u3a, 3, 0, KA), (u3b, 3, KA, KB))
        return [load_u(*place, n) for n, place in enumerate(places)]

    load_f(0, 0, 0).start()
    load_uo(xo, 0).start()
    load_uo(xp, 0).start()

    def follow(src, dst, n):
        return pltpu.make_async_remote_copy(
            src_ref=src, dst_ref=dst.at[pl.ds(SD, SD)],
            send_sem=y_s.at[0], recv_sem=y_r.at[n], device_id=before, device_id_type=MESH,
        )

    follow0 = follow(uo.at[0], u0, 0)
    follow1 = follow(uo.at[1], u1, 1)
    follow2a = follow(uo.at[2, :, pl.ds(0, KA)], u2a, 2)
    follow2b = follow(uo.at[2, :, pl.ds(KA, KB)], u2b, 3)
    follow3a = follow(uo.at[3, :, pl.ds(0, KA)], u3a, 4)
    follow3b = follow(uo.at[3, :, pl.ds(KA, KB)], u3b, 5)

    def hop1(i):
        return pltpu.make_async_remote_copy(
            src_ref=uo.at[3, :, pl.ds(i * KB, KB)], dst_ref=yb1.at[i],
            send_sem=y_s.at[0], recv_sem=l1_r.at[i], device_id=hop_to, device_id_type=MESH,
        )

    def hop2(i):
        return pltpu.make_async_remote_copy(
            src_ref=yb1.at[i], dst_ref=yb2.at[i],
            send_sem=y_s.at[0], recv_sem=l2_r.at[i], device_id=hop_to, device_id_type=MESH,
        )

    def turn(i):
        return pltpu.make_async_remote_copy(
            src_ref=yb2.at[i], dst_ref=yb3.at[i],
            send_sem=t_s.at[0], recv_sem=t_r.at[i], device_id=row_to, device_id_type=MESH,
        )

    def end(i, src):
        if i < LP - 1:
            target = u3a.at[pl.ds(SD, SD), pl.ds(i * KB, KB)]
        else:
            target = u3b.at[pl.ds(SD, SD)]
        return pltpu.make_async_remote_copy(
            src_ref=src.at[i], dst_ref=target,
            send_sem=y_s.at[0], recv_sem=l3_r.at[i], device_id=end_to, device_id_type=MESH,
        )

    H = W // 2

    def direct(b, k):
        return pltpu.make_async_remote_copy(
            src_ref=half.at[b, (xp, xm)[k]], dst_ref=hr.at[b, me],
            send_sem=x_s.at[0], recv_sem=x_r.at[b],
            device_id=(right, left)[k], device_id_type=MESH,
        )

    def relay1(b, k):
        return pltpu.make_async_remote_copy(
            src_ref=half.at[b, xo, pl.ds(k * H, H)], dst_ref=rbuf.at[b, k],
            send_sem=x_s.at[0], recv_sem=r1_r.at[b, k],
            device_id=(right, left)[k], device_id_type=MESH,
        )

    def relay2(b, k):
        return pltpu.make_async_remote_copy(
            src_ref=rbuf.at[b, k], dst_ref=hr.at[b, (xm, xp)[k], pl.ds(k * H, H)],
            send_sem=x_s.at[0], recv_sem=x_r.at[b],
            device_id=(right, left)[k], device_id_type=MESH,
        )

    def first_product(b, q, d):
        return lax.dot_general(
            uo[d, q], fer[b], (((0,), (0,)), ((), ())), preferred_element_type=jnp.float32
        ).astype(jnp.bfloat16)

    load_f(0, 0, 0).wait()
    load_uo(xo, 0).wait()
    for j in (xm, me):
        load_uo(j, 0).start()
    for j in (0, 3, 1, 2):
        load_uo(j, 1).start()
    for f in range(1, FL):
        load_f(f, f, 0).start()
    for f in range(FL):
        load_f(FL + f, f, 1).start()
    half[0, xo] = first_product(0, 0, xo)
    load_uo(xp, 0).wait()
    half[0, xp] = first_product(0, 0, xp)

    @pl.when(core == 1)
    def _():
        pl.semaphore_wait(barrier, 5)

    @pl.when((core == 0) & turns)
    def _():
        pl.semaphore_wait(barrier, 9)

    @pl.when((core == 0) & jnp.logical_not(turns))
    def _():
        pl.semaphore_wait(barrier, 7)

    relay1(0, 0).start()
    relay1(0, 1).start()
    load_uo(xm, 0).wait()
    load_uo(me, 0).wait()
    load_uo(0, 1).wait()

    @pl.when(core == 0)
    def _():
        follow0.start()

    load_uo(3, 1).wait()

    @pl.when(core == 0)
    def _():
        for i in range(LP):
            hop1(i).start()

    half[0, xm] = first_product(0, 0, xm)
    direct(0, 0).start()
    hr[0, me] = first_product(0, 0, me)
    direct(0, 1).start()
    load_uo(1, 1).wait()
    load_uo(2, 1).wait()

    @pl.when(core == 0)
    def _():
        follow1.start()
        follow2a.start()
        follow2b.start()

    def stage1(b, _):
        q = b // FL
        load_f(b, 0, 0).wait()
        half[b, xo] = first_product(b, q, xo)
        half[b, xp] = first_product(b, q, xp)
        relay1(b, 0).start()
        relay1(b, 1).start()
        half[b, xm] = first_product(b, q, xm)
        direct(b, 0).start()
        hr[b, me] = first_product(b, q, me)
        direct(b, 1).start()
        return 0

    lax.fori_loop(1, B, stage1, 0)
    for copy in own_u():
        copy.start()

    @pl.when(core == 1)
    def _():
        for copy in (follow0, follow1, follow2a, follow2b, follow3a, follow3b):
            copy.start()

    def forward_x(b):
        for k in range(2):
            relay1(b, k).wait_recv()
            relay2(b, k).start()

    def forward_y1(i):
        @pl.when(core == 0)
        def _():
            hop1(i).wait_recv()
            hop2(i).start()

    def forward_y2(i):
        @pl.when(core == 0)
        def _():
            hop2(i).wait_recv()

            @pl.when(turns)
            def _():
                turn(i).start()

            @pl.when(jnp.logical_not(turns))
            def _():
                end(i, yb2).start()

    def forward_end(i):
        @pl.when((core == 0) & turns)
        def _():
            turn(i).wait_recv()
            end(i, yb3).start()

    forward_y1(0)
    forward_x(0)
    forward_y1(1)
    forward_x(1)
    forward_y1(2)
    forward_x(2)
    forward_y1(3)
    forward_x(3)
    forward_y2(0)
    forward_y2(1)
    forward_end(0)
    forward_x(4)
    forward_y2(2)
    forward_end(1)
    forward_x(5)
    forward_y2(3)
    forward_end(2)
    forward_end(3)

    for copy in own_u():
        copy.wait()

    def locate(b):
        q = b // FL
        f = b - q * FL
        return f, q, lax.rem(partner[q, f] - first_sector + SECS * SD, 2 * SD)

    def rows_of(b, low, high):
        return jnp.concatenate([hr[b, s] for s in range(low, high)], axis=1)

    def times(rows, ref, index):
        return jnp.dot(rows, ref[index], preferred_element_type=jnp.float32)

    def arrive(b):
        here = hr.at[b, pl.ds(0, NS - 1)]
        pltpu.make_async_copy(here, here, x_r.at[b]).wait()

    def whole(b):
        f, q, index = locate(b)
        rows = rows_of(b, 0, NS)
        out[f, q, :, 0:W] = times(rows, u0, index).astype(jnp.bfloat16)
        out[f, q, :, W:2 * W] = times(rows, u1, index).astype(jnp.bfloat16)

    def part(b):
        f, q, index = locate(b)
        rows = rows_of(b, 0, NS - 1)
        acc[b, 0] = times(rows, u2a, index)
        acc[b, 1] = times(rows, u3a, index)

    def rest(b):
        f, q, index = locate(b)
        rows = hr[b, NS - 1]
        out[f, q, :, 2 * W:3 * W] = (acc[b, 0] + times(rows, u2b, index)).astype(jnp.bfloat16)
        out[f, q, :, 3 * W:4 * W] = (acc[b, 1] + times(rows, u3b, index)).astype(jnp.bfloat16)

    def early(b, _):
        arrive(b)
        whole(b)
        return 0

    def middle(b, _):
        part(b)
        return 0

    def late(b, _):
        arrive(b)
        whole(b)
        part(b)
        return 0

    def last(b, _):
        rest(b)
        return 0

    follow0.wait_recv()
    follow1.wait_recv()
    lax.fori_loop(0, B - 2, early, 0)
    follow2a.wait_recv()

    @pl.when(core == 0)
    def _():
        follow3a.wait_recv()

    @pl.when(core == 1)
    def _():
        for i in range(LP - 1):
            end(i, yb2).wait_recv()

    lax.fori_loop(0, B - 2, middle, 0, unroll=True)
    lax.fori_loop(B - 2, B, late, 0)
    follow2b.wait_recv()

    @pl.when(core == 0)
    def _():
        follow3b.wait_recv()

    @pl.when(core == 1)
    def _():
        end(LP - 1, yb2).wait_recv()

    lax.fori_loop(0, B, last, 0, unroll=True)

    pltpu.make_async_copy(hr, hr, x_s.at[0]).wait()

    @pl.when(core == 0)
    def _():
        pltpu.make_async_copy(fer, fer, y_s.at[0]).wait()
        pltpu.make_async_copy(half, half, y_s.at[0]).wait()

        @pl.when(turns)
        def _():
            pltpu.make_async_copy(yb2, yb2, t_s.at[0]).wait()

    @pl.when(core == 1)
    def _():
        pltpu.make_async_copy(uo, uo, y_s.at[0]).wait()


def write_out(result, out, sems):
    copies = [
        pltpu.make_async_copy(result.at[b // SD, b % SD], out.at[b // SD, b % SD], sems.at[b])
        for b in range(B)
    ]
    for copy in copies:
        copy.start()
    for copy in copies:
        copy.wait()


def local(basis, fermion, partner):
    bf16 = jnp.bfloat16
    dma = pltpu.SemaphoreType.DMA
    result = pl.pallas_call(
        kernel,
        out_shape=pltpu.VMEM((FL, SD, W, NB), bf16),
        in_specs=[
            pl.BlockSpec(memory_space=pltpu.HBM),
            pl.BlockSpec(memory_space=pltpu.HBM),
            pl.BlockSpec(memory_space=pltpu.SMEM),
        ],
        out_specs=pl.BlockSpec(memory_space=pltpu.VMEM),
        scratch_shapes=[
            pltpu.VMEM((NS, SD, NB, W), bf16),
            pltpu.VMEM((2 * SD, NB, W), bf16),
            pltpu.VMEM((2 * SD, NB, W), bf16),
            pltpu.VMEM((2 * SD, KA, W), bf16),
            pltpu.VMEM((2 * SD, KB, W), bf16),
            pltpu.VMEM((2 * SD, KA, W), bf16),
            pltpu.VMEM((2 * SD, KB, W), bf16),
            pltpu.VMEM((B, NB, W), bf16),
            pltpu.VMEM((B, NS, W, W), bf16),
            pltpu.VMEM((B, NS, W, W), bf16),
            pltpu.VMEM((B, 2, W // 2, W), bf16),
            pltpu.VMEM((LP, SD, KB, W), bf16),
            pltpu.VMEM((LP, SD, KB, W), bf16),
            pltpu.VMEM((LP, SD, KB, W), bf16),
            pltpu.VMEM((B, 2, W, W), jnp.float32),
            dma((NS, SD)), dma((B,)), dma((6,)),
            dma((1,)), dma((B,)), dma((B, 2)),
            dma((1,)), dma((6,)), dma((LP,)), dma((LP,)), dma((LP,)), dma((1,)), dma((LP,)),
        ],
        compiler_params=pltpu.CompilerParams(
            collective_id=0, has_side_effects=True, vmem_limit_bytes=56 * 2**20
        ),
    )(basis, fermion, partner.T)
    return pl.pallas_call(
        write_out,
        out_shape=jax.ShapeDtypeStruct((FL, SD, W, NB), bf16),
        in_specs=[pl.BlockSpec(memory_space=pltpu.VMEM)],
        out_specs=pl.BlockSpec(memory_space=pl.ANY),
        scratch_shapes=[dma((B,))],
        compiler_params=pltpu.CompilerParams(vmem_limit_bytes=2**20),
    )(result)


def solution(mesh):
    placed = (P("sec", None, None), P(None, "sec", None, "slab"), P(None, "sec"))
    return jax.shard_map(
        local, mesh=mesh, in_specs=placed, out_specs=P(None, "sec", "slab", None), check_vma=False
    )
```

time: 81.4 us -> 47.2 us (0.58)
  the two profiles are of different devices: /device:TPU:115 before, /device:TPU:9 now
where the time goes in v2:
time: 47.2 us; the launch traced here: 47 us
  Pallas kernels  47 us (100%)
    pallas_call x1, Pallas kernels, local(): pl.pallas_call(kernel, out_shape=pltpu.VMEM((FL, SD, W, NB), bf16), in_sp...  45.3 us
    pallas_call x1, Pallas kernels, local(): pl.pallas_call(write_out, out_shape=jax.ShapeDtypeStruct((FL, SD, W, NB),...  1.71 us

profile of v2, /device:TPU:9, one launch (start us, length us, event | category | flops | bytes accessed | tf_op | source)
XLA Modules:
  0.0 47.0 jit_solution(11716796632271225053)
XLA Ops:
  0.0 45.3 %shard_map.37.result = bf16[3,2,256,1024]{3,2,1,0:T(8,128)(2,1)S(1)} custom-call(bf16[2,1024,1024]{2,1,0:T(8,128)(2,1)} %basis.1, bf16[3,2,1024,256]{3,2,1,0:T(8,128)(2,1)} %fermion.1, s32[2,3]{1,0:T(2,128)} %bitcast.1), custom_call_target="tpu_custom_call" | custom-call | tf_op jit(solution)/shard_map/pallas_call | solution.py:405
  45.3 1.7 %shard_map.38 = bf16[3,2,256,1024]{3,2,1,0:T(8,128)(2,1)} custom-call(bf16[3,2,256,1024]{3,2,1,0:T(8,128)(2,1)S(1)} %shard_map.37.result), custom_call_target="tpu_custom_call" | custom-call | tf_op jit(solution)/shard_map/pallas_call | solution.py:438

commit v3 on v2

--- a/solution.py
+++ b/solution.py
@@ -22,9 +22,9 @@
 
 
 def kernel(
-    basis, fermion, partner, out,
+    basis, fermion, partner_in, out,
     uo, u0, u1, u2a, u2b, u3a, u3b, fer, half, hr, rbuf, yb1, yb2, yb3, acc,
-    lu, lf, lo, x_s, x_r, r1_r, y_s, y_r, l1_r, l2_r, l3_r, t_s, t_r,
+    lu, lf, lo, x_s, x_r, r1_r, y_s, y_r, l1_r, l2_r, l3_r, t_s, t_r, answer, partner, p_s,
 ):
     sec = lax.axis_index("sec")
     me = lax.axis_index("slab")
@@ -49,27 +49,44 @@
     turns = y == 2
     first_sector = sec * SD
 
+    head = (core == 0) & (y == 0) & (z == 0)
+    head_peer = (core == 1) & (y == NY - 1) & (z == nz - 1)
+    turn_head = (core == 0) & turns & (z == 0)
+    turn_peer = (core == 0) & turns & (z == nz - 1)
+    passes = (core == 0) & (y == 1) & (z == 0)
+    spare = (core == 0) & (y == 3) & (z == 0)
+    spare_to = (core == 1) & (y == 2) & (z == 0)
     barrier = pltpu.get_barrier_semaphore()
 
     def greet(device):
         pl.semaphore_signal(barrier, inc=1, device_id=device, device_id_type=MESH)
 
-    for device in (right, left, before, after):
-        greet(device)
+    greet(right)
+    greet(left)
+
+    @pl.when(jnp.logical_not(head_peer))
+    def _():
+        greet(after)
 
     @pl.when(core == 0)
     def _():
-        for device in (hop_to, hop_from, end_to):
-            greet(device)
-
-        @pl.when(turns)
-        def _():
-            greet(row_to)
-            greet(row_from)
+        greet(hop_from)
 
     @pl.when(core == 1)
     def _():
         greet(end_from)
+
+    @pl.when((core == 0) & turns & (z != nz - 1))
+    def _():
+        greet(row_from)
+
+    @pl.when(head)
+    def _():
+        greet(before)
+
+    @pl.when(turn_head)
+    def _():
+        greet(row_to)
 
     def load_uo(j, q):
         return pltpu.make_async_copy(
@@ -89,9 +106,11 @@
                   (u3a, 3, 0, KA), (u3b, 3, KA, KB))
         return [load_u(*place, n) for n, place in enumerate(places)]
 
+    load_partner = pltpu.make_async_copy(partner_in, partner, p_s.at[0])
     load_f(0, 0, 0).start()
     load_uo(xo, 0).start()
     load_uo(xp, 0).start()
+    load_partner.start()
 
     def follow(src, dst, n):
         return pltpu.make_async_remote_copy(
@@ -99,16 +118,20 @@
             send_sem=y_s.at[0], recv_sem=y_r.at[n], device_id=before, device_id_type=MESH,
         )
 
-    follow0 = follow(uo.at[0], u0, 0)
-    follow1 = follow(uo.at[1], u1, 1)
-    follow2a = follow(uo.at[2, :, pl.ds(0, KA)], u2a, 2)
-    follow2b = follow(uo.at[2, :, pl.ds(KA, KB)], u2b, 3)
-    follow3a = follow(uo.at[3, :, pl.ds(0, KA)], u3a, 4)
-    follow3b = follow(uo.at[3, :, pl.ds(KA, KB)], u3b, 5)
+    follow0 = follow(basis.at[:, :, pl.ds(0, W)], u0, 0)
+    follow1 = follow(basis.at[:, :, pl.ds(W, W)], u1, 1)
+    follow2a = follow(basis.at[:, pl.ds(0, KA), pl.ds(2 * W, W)], u2a, 2)
+    follow2b = follow(basis.at[:, pl.ds(KA, KB), pl.ds(2 * W, W)], u2b, 3)
+    follow3a = follow(basis.at[:, pl.ds(0, KA), pl.ds(3 * W, W)], u3a, 4)
+    follow3b = follow(basis.at[:, pl.ds(KA, KB), pl.ds(3 * W, W)], u3b, 5)
 
     def hop1(i):
-        return pltpu.make_async_remote_copy(
-            src_ref=uo.at[3, :, pl.ds(i * KB, KB)], dst_ref=yb1.at[i],
+        if i < LP:
+            source = basis.at[:, pl.ds(i * KB, KB), pl.ds(3 * W, W)]
+        else:
+            source = basis.at[:, pl.ds(KA, KB), pl.ds(2 * W, W)]
+        return pltpu.make_async_remote_copy(
+            src_ref=source, dst_ref=yb1.at[i],
             send_sem=y_s.at[0], recv_sem=l1_r.at[i], device_id=hop_to, device_id_type=MESH,
         )
 
@@ -128,7 +151,7 @@
         if i < LP - 1:
             target = u3a.at[pl.ds(SD, SD), pl.ds(i * KB, KB)]
         else:
-            target = u3b.at[pl.ds(SD, SD)]
+            target = (u3b if i == LP - 1 else u2b).at[pl.ds(SD, SD)]
         return pltpu.make_async_remote_copy(
             src_ref=src.at[i], dst_ref=target,
             send_sem=y_s.at[0], recv_sem=l3_r.at[i], device_id=end_to, device_id_type=MESH,
@@ -161,6 +184,48 @@
         return lax.dot_general(
             uo[d, q], fer[b], (((0,), (0,)), ((), ())), preferred_element_type=jnp.float32
         ).astype(jnp.bfloat16)
+
+    def one(condition):
+        return jnp.where(condition, 1, 0)
+
+    greeted = jnp.where(
+        core == 1, 3 + one(head_peer), 5 - one(head) + one(turns & (z != 0)) + one(turn_peer)
+    )
+    pl.semaphore_wait(barrier, greeted)
+
+    @pl.when(turn_peer)
+    def _():
+        pl.semaphore_signal(answer, inc=1, device_id=row_from, device_id_type=MESH)
+
+    @pl.when(head_peer)
+    def _():
+        pl.semaphore_signal(answer, inc=1, device_id=after, device_id_type=MESH)
+
+    def send_chunks():
+        for copy in (follow0, follow1, follow2a):
+            copy.start()
+
+    @pl.when((core == 0) & jnp.logical_not(head))
+    def _():
+        send_chunks()
+        follow2b.start()
+
+    @pl.when(spare)
+    def _():
+        follow3b.start()
+
+    @pl.when(core == 0)
+    def _():
+        for i in range(LP - 1):
+            hop1(i).start()
+
+    @pl.when((core == 0) & jnp.logical_not(spare))
+    def _():
+        hop1(LP - 1).start()
+
+    @pl.when(head)
+    def _():
+        hop1(LP).start()
 
     load_f(0, 0, 0).wait()
     load_uo(xo, 0).wait()
@@ -172,51 +237,23 @@
         load_f(f, f, 0).start()
     for f in range(FL):
         load_f(FL + f, f, 1).start()
-    half[0, xo] = first_product(0, 0, xo)
+    for k in range(2):
+        half[0, xo, k * H:(k + 1) * H] = lax.dot_general(
+            uo[xo, 0, :, k * H:(k + 1) * H], fer[0], (((0,), (0,)), ((), ())),
+            preferred_element_type=jnp.float32,
+        ).astype(jnp.bfloat16)
+    relay1(0, 0).start()
     load_uo(xp, 0).wait()
     half[0, xp] = first_product(0, 0, xp)
-
-    @pl.when(core == 1)
-    def _():
-        pl.semaphore_wait(barrier, 5)
-
-    @pl.when((core == 0) & turns)
-    def _():
-        pl.semaphore_wait(barrier, 9)
-
-    @pl.when((core == 0) & jnp.logical_not(turns))
-    def _():
-        pl.semaphore_wait(barrier, 7)
-
-    relay1(0, 0).start()
     relay1(0, 1).start()
     load_uo(xm, 0).wait()
-    load_uo(me, 0).wait()
-    load_uo(0, 1).wait()
-
-    @pl.when(core == 0)
-    def _():
-        follow0.start()
-
-    load_uo(3, 1).wait()
-
-    @pl.when(core == 0)
-    def _():
-        for i in range(LP):
-            hop1(i).start()
-
     half[0, xm] = first_product(0, 0, xm)
     direct(0, 0).start()
+    load_uo(me, 0).wait()
     hr[0, me] = first_product(0, 0, me)
     direct(0, 1).start()
-    load_uo(1, 1).wait()
-    load_uo(2, 1).wait()
-
-    @pl.when(core == 0)
-    def _():
-        follow1.start()
-        follow2a.start()
-        follow2b.start()
+    for j in range(NS):
+        load_uo(j, 1).wait()
 
     def stage1(b, _):
         q = b // FL
@@ -231,7 +268,14 @@
         direct(b, 1).start()
         return 0
 
-    lax.fori_loop(1, B, stage1, 0)
+    lax.fori_loop(1, 4, stage1, 0)
+
+    @pl.when(head)
+    def _():
+        pl.semaphore_wait(answer, 1)
+        send_chunks()
+
+    lax.fori_loop(4, B, stage1, 0)
     for copy in own_u():
         copy.start()
 
@@ -246,26 +290,35 @@
             relay2(b, k).start()
 
     def forward_y1(i):
-        @pl.when(core == 0)
+        here = (core == 0, (core == 0) & jnp.logical_not(head), passes)[max(0, i - LP + 2)]
+
+        @pl.when(here)
         def _():
             hop1(i).wait_recv()
             hop2(i).start()
 
     def forward_y2(i):
-        @pl.when(core == 0)
+        here = (core == 0, (core == 0) & jnp.logical_not(passes), turn_head)[max(0, i - LP + 2)]
+
+        @pl.when(here)
         def _():
             hop2(i).wait_recv()
+            if i == 0:
+                @pl.when(turn_head)
+                def _():
+                    pl.semaphore_wait(answer, 1)
 
             @pl.when(turns)
             def _():
                 turn(i).start()
 
-            @pl.when(jnp.logical_not(turns))
-            def _():
-                end(i, yb2).start()
+            if i < LP:
+                @pl.when(jnp.logical_not(turns))
+                def _():
+                    end(i, yb2).start()
 
     def forward_end(i):
-        @pl.when((core == 0) & turns)
+        @pl.when((core == 0) & turns if i < LP else turn_peer)
         def _():
             turn(i).wait_recv()
             end(i, yb3).start()
@@ -275,20 +328,24 @@
     forward_y1(1)
     forward_x(1)
     forward_y1(2)
+    forward_y1(3)
     forward_x(2)
-    forward_y1(3)
+    forward_y2(0)
+    forward_y1(4)
     forward_x(3)
-    forward_y2(0)
     forward_y2(1)
     forward_end(0)
+    forward_y2(2)
     forward_x(4)
-    forward_y2(2)
     forward_end(1)
-    forward_x(5)
     forward_y2(3)
     forward_end(2)
+    forward_x(5)
+    forward_y2(4)
     forward_end(3)
-
+    forward_end(4)
+
+    load_partner.wait()
     for copy in own_u():
         copy.wait()
 
@@ -359,44 +416,55 @@
             end(i, yb2).wait_recv()
 
     lax.fori_loop(0, B - 2, middle, 0, unroll=True)
-    lax.fori_loop(B - 2, B, late, 0)
-    follow2b.wait_recv()
+    lax.fori_loop(B - 2, B, late, 0, unroll=True)
+
+    @pl.when(jnp.logical_not(head_peer))
+    def _():
+        follow2b.wait_recv()
+
+    @pl.when(head_peer)
+    def _():
+        end(LP, yb2).wait_recv()
+
+    @pl.when((core == 0) | spare_to)
+    def _():
+        follow3b.wait_recv()
+
+    @pl.when((core == 1) & jnp.logical_not(spare_to))
+    def _():
+        end(LP - 1, yb2).wait_recv()
+
+    lax.fori_loop(0, B, last, 0, unroll=True)
+
+    def sent(ref, sem):
+        pltpu.make_async_copy(ref, ref, sem.at[0]).wait()
+
+    sent(hr, x_s)
 
     @pl.when(core == 0)
     def _():
-        follow3b.wait_recv()
+        sent(fer, y_s)
+        sent(half.at[pl.ds(0, B - 1)], y_s)
+
+        @pl.when(jnp.logical_not(head))
+        def _():
+            sent(half.at[0], y_s)
+
+        @pl.when(head | turn_peer)
+        def _():
+            sent(half.at[0, pl.ds(0, 2)], y_s)
+
+        @pl.when(turns)
+        def _():
+            sent(yb2.at[pl.ds(0, LP)], t_s)
+
+        @pl.when(turn_head)
+        def _():
+            sent(yb2.at[LP], t_s)
 
     @pl.when(core == 1)
     def _():
-        end(LP - 1, yb2).wait_recv()
-
-    lax.fori_loop(0, B, last, 0, unroll=True)
-
-    pltpu.make_async_copy(hr, hr, x_s.at[0]).wait()
-
-    @pl.when(core == 0)
-    def _():
-        pltpu.make_async_copy(fer, fer, y_s.at[0]).wait()
-        pltpu.make_async_copy(half, half, y_s.at[0]).wait()
-
-        @pl.when(turns)
-        def _():
-            pltpu.make_async_copy(yb2, yb2, t_s.at[0]).wait()
-
-    @pl.when(core == 1)
-    def _():
-        pltpu.make_async_copy(uo, uo, y_s.at[0]).wait()
-
-
-def write_out(result, out, sems):
-    copies = [
-        pltpu.make_async_copy(result.at[b // SD, b % SD], out.at[b // SD, b % SD], sems.at[b])
-        for b in range(B)
-    ]
-    for copy in copies:
-        copy.start()
-    for copy in copies:
-        copy.wait()
+        sent(uo, y_s)
 
 
 def local(basis, fermion, partner):
@@ -408,7 +476,7 @@
         in_specs=[
             pl.BlockSpec(memory_space=pltpu.HBM),
             pl.BlockSpec(memory_space=pltpu.HBM),
-            pl.BlockSpec(memory_space=pltpu.SMEM),
+            pl.BlockSpec(memory_space=pltpu.HBM),
         ],
         out_specs=pl.BlockSpec(memory_space=pltpu.VMEM),
         scratch_shapes=[
@@ -423,26 +491,20 @@
             pltpu.VMEM((B, NS, W, W), bf16),
             pltpu.VMEM((B, NS, W, W), bf16),
             pltpu.VMEM((B, 2, W // 2, W), bf16),
-            pltpu.VMEM((LP, SD, KB, W), bf16),
-            pltpu.VMEM((LP, SD, KB, W), bf16),
-            pltpu.VMEM((LP, SD, KB, W), bf16),
+            pltpu.VMEM((LP + 1, SD, KB, W), bf16),
+            pltpu.VMEM((LP + 1, SD, KB, W), bf16),
+            pltpu.VMEM((LP + 1, SD, KB, W), bf16),
             pltpu.VMEM((B, 2, W, W), jnp.float32),
             dma((NS, SD)), dma((B,)), dma((6,)),
             dma((1,)), dma((B,)), dma((B, 2)),
-            dma((1,)), dma((6,)), dma((LP,)), dma((LP,)), dma((LP,)), dma((1,)), dma((LP,)),
+            dma((1,)), dma((6,)), *[dma((LP + 1,)) for _ in range(3)], dma((1,)), dma((LP + 1,)), pltpu.SemaphoreType.REGULAR,
+            pltpu.SMEM((SD, FL), jnp.int32), dma((1,)),
         ],
         compiler_params=pltpu.CompilerParams(
             collective_id=0, has_side_effects=True, vmem_limit_bytes=56 * 2**20
         ),
     )(basis, fermion, partner.T)
-    return pl.pallas_call(
-        write_out,
-        out_shape=jax.ShapeDtypeStruct((FL, SD, W, NB), bf16),
-        in_specs=[pl.BlockSpec(memory_space=pltpu.VMEM)],
-        out_specs=pl.BlockSpec(memory_space=pl.ANY),
-        scratch_shapes=[dma((B,))],
-        compiler_params=pltpu.CompilerParams(vmem_limit_bytes=2**20),
-    )(result)
+    return result
 
 
 def solution(mesh):

time: 47.2 us -> 45.3 us (0.960)
  the two profiles are of different devices: /device:TPU:9 before, /device:TPU:249 now
where the time goes in v3:
time: 45.3 us; the launch traced here: 44.9 us
  Pallas kernels  43.3 us (96%)
  local copies, waits for them, and re-layouts  1.67 us (4%)
    pallas_call x1, Pallas kernels, local(): pl.pallas_call(kernel, out_shape=pltpu.VMEM((FL, SD, W, NB), bf16), in_sp...  43.3 us
    unnamed x1, local copies, waits for them, and re-layouts  1.67 us

profile of v3, /device:TPU:249, one launch (start us, length us, event | category | flops | bytes accessed | tf_op | source)
XLA Modules:
  0.0 44.9 jit_solution(9779761804778154220)
XLA Ops:
  0.0 43.3 %shard_map.37 = bf16[3,2,256,1024]{3,2,1,0:T(8,128)(2,1)S(1)} custom-call(bf16[2,1024,1024]{2,1,0:T(8,128)(2,1)} %basis.1, bf16[3,2,1024,256]{3,2,1,0:T(8,128)(2,1)} %fermion.1, s32[2,3]{1,0:T(2,128)} %bitcast.1), custom_call_target="tpu_custom_call" | custom-call | tf_op jit(solution)/shard_map/pallas_call | solution.py:473
  43.3 1.7 %copy.5 = bf16[3,2,256,1024]{3,2,1,0:T(8,128)(2,1)} copy(bf16[3,2,256,1024]{3,2,1,0:T(8,128)(2,1)S(1)} %shard_map.37) | data formatting | bytes 6291456

commit v4 on v3

--- a/solution.py
+++ b/solution.py
@@ -19,6 +19,7 @@
 LP = 4
 KB = NB // LP
 KA = NB - KB
+KH = KB // 2
 
 
 def kernel(
@@ -90,21 +91,21 @@
 
     def load_uo(j, q):
         return pltpu.make_async_copy(
-            basis.at[q, :, pl.ds(pl.multiple_of(j * W, W), W)], uo.at[j, q], lu.at[j, q]
+            basis.at[q, :, pl.ds(pl.multiple_of(j * W, W), W)], uo.at[j, q], lu.at[j if q == 0 else NS]
         )
 
     def load_f(b, f, q):
         return pltpu.make_async_copy(fermion.at[f, q], fer.at[b], lf.at[b])
 
-    def load_u(ref, j, row, rows, n):
+    def load_u(ref, j, row, rows):
         return pltpu.make_async_copy(
-            basis.at[:, pl.ds(row, rows), pl.ds(j * W, W)], ref.at[pl.ds(0, SD)], lo.at[n]
+            basis.at[:, pl.ds(row, rows), pl.ds(j * W, W)], ref.at[pl.ds(0, SD)], lo.at[0]
         )
 
     def own_u():
         places = ((u0, 0, 0, NB), (u1, 1, 0, NB), (u2a, 2, 0, KA), (u2b, 2, KA, KB),
                   (u3a, 3, 0, KA), (u3b, 3, KA, KB))
-        return [load_u(*place, n) for n, place in enumerate(places)]
+        return [load_u(*place) for place in places]
 
     load_partner = pltpu.make_async_copy(partner_in, partner, p_s.at[0])
     load_f(0, 0, 0).start()
@@ -125,19 +126,25 @@
     follow3a = follow(basis.at[:, pl.ds(0, KA), pl.ds(3 * W, W)], u3a, 4)
     follow3b = follow(basis.at[:, pl.ds(KA, KB), pl.ds(3 * W, W)], u3b, 5)
 
-    def hop1(i):
+    follow3c = pltpu.make_async_remote_copy(
+        src_ref=basis.at[:, pl.ds(KA + KH, KH), pl.ds(3 * W, W)],
+        dst_ref=u3b.at[pl.ds(SD, SD), pl.ds(KH, KH)],
+        send_sem=y_s.at[0], recv_sem=y_r.at[5], device_id=before, device_id_type=MESH,
+    )
+
+    def hop1(i, rows=KB):
         if i < LP:
-            source = basis.at[:, pl.ds(i * KB, KB), pl.ds(3 * W, W)]
+            source = basis.at[:, pl.ds(i * KB, rows), pl.ds(3 * W, W)]
         else:
             source = basis.at[:, pl.ds(KA, KB), pl.ds(2 * W, W)]
         return pltpu.make_async_remote_copy(
-            src_ref=source, dst_ref=yb1.at[i],
+            src_ref=source, dst_ref=yb1.at[i, :, pl.ds(0, rows)],
             send_sem=y_s.at[0], recv_sem=l1_r.at[i], device_id=hop_to, device_id_type=MESH,
         )
 
-    def hop2(i):
-        return pltpu.make_async_remote_copy(
-            src_ref=yb1.at[i], dst_ref=yb2.at[i],
+    def hop2(i, rows=KB):
+        return pltpu.make_async_remote_copy(
+            src_ref=yb1.at[i, :, pl.ds(0, rows)], dst_ref=yb2.at[i, :, pl.ds(0, rows)],
             send_sem=y_s.at[0], recv_sem=l2_r.at[i], device_id=hop_to, device_id_type=MESH,
         )
 
@@ -147,14 +154,14 @@
             send_sem=t_s.at[0], recv_sem=t_r.at[i], device_id=row_to, device_id_type=MESH,
         )
 
-    def end(i, src):
+    def end(i, src, rows=KB):
         if i < LP - 1:
             target = u3a.at[pl.ds(SD, SD), pl.ds(i * KB, KB)]
         else:
-            target = (u3b if i == LP - 1 else u2b).at[pl.ds(SD, SD)]
-        return pltpu.make_async_remote_copy(
-            src_ref=src.at[i], dst_ref=target,
-            send_sem=y_s.at[0], recv_sem=l3_r.at[i], device_id=end_to, device_id_type=MESH,
+            target = (u3b if i == LP - 1 else u2b).at[pl.ds(SD, SD), pl.ds(0, rows)]
+        return pltpu.make_async_remote_copy(
+            src_ref=src.at[i, :, pl.ds(0, rows)], dst_ref=target,
+            send_sem=y_s.at[0], recv_sem=l3_r.at[max(0, i - LP + 2)], device_id=end_to, device_id_type=MESH,
         )
 
     H = W // 2
@@ -169,7 +176,7 @@
     def relay1(b, k):
         return pltpu.make_async_remote_copy(
             src_ref=half.at[b, xo, pl.ds(k * H, H)], dst_ref=rbuf.at[b, k],
-            send_sem=x_s.at[0], recv_sem=r1_r.at[b, k],
+            send_sem=x_s.at[0], recv_sem=r1_r.at[b],
             device_id=(right, left)[k], device_id_type=MESH,
         )
 
@@ -212,7 +219,7 @@
 
     @pl.when(spare)
     def _():
-        follow3b.start()
+        follow3c.start()
 
     @pl.when(core == 0)
     def _():
@@ -222,6 +229,10 @@
     @pl.when((core == 0) & jnp.logical_not(spare))
     def _():
         hop1(LP - 1).start()
+
+    @pl.when(spare)
+    def _():
+        hop1(LP - 1, KH).start()
 
     @pl.when(head)
     def _():
@@ -252,8 +263,8 @@
     load_uo(me, 0).wait()
     hr[0, me] = first_product(0, 0, me)
     direct(0, 1).start()
-    for j in range(NS):
-        load_uo(j, 1).wait()
+    second = uo.at[:, 1]
+    pltpu.make_async_copy(second, second, lu.at[NS]).wait()
 
     def stage1(b, _):
         q = b // FL
@@ -285,22 +296,35 @@
             copy.start()
 
     def forward_x(b):
+        pltpu.make_async_copy(rbuf.at[b], rbuf.at[b], r1_r.at[b]).wait()
         for k in range(2):
-            relay1(b, k).wait_recv()
             relay2(b, k).start()
 
     def forward_y1(i):
-        here = (core == 0, (core == 0) & jnp.logical_not(head), passes)[max(0, i - LP + 2)]
-
-        @pl.when(here)
-        def _():
-            hop1(i).wait_recv()
-            hop2(i).start()
+        short = (i == LP - 1) & head
+        if i < LP:
+            @pl.when((core == 0) & jnp.logical_not(short))
+            def _():
+                hop1(i).wait_recv()
+                hop2(i).start()
+
+        if i >= LP - 1:
+            rows = KH if i == LP - 1 else KB
+
+            @pl.when(short if i == LP - 1 else passes)
+            def _():
+                hop1(i, rows).wait_recv()
+                hop2(i, rows).start()
 
     def forward_y2(i):
-        here = (core == 0, (core == 0) & jnp.logical_not(passes), turn_head)[max(0, i - LP + 2)]
-
-        @pl.when(here)
+        short = (i == LP - 1) & passes
+        if i < LP:
+            @pl.when((core == 0) & jnp.logical_not(turns | short))
+            def _():
+                hop2(i).wait_recv()
+                end(i, yb2).start()
+
+        @pl.when((core == 0) & turns if i < LP else turn_head)
         def _():
             hop2(i).wait_recv()
             if i == 0:
@@ -308,14 +332,13 @@
                 def _():
                     pl.semaphore_wait(answer, 1)
 
-            @pl.when(turns)
+            turn(i).start()
+
+        if i == LP - 1:
+            @pl.when(passes)
             def _():
-                turn(i).start()
-
-            if i < LP:
-                @pl.when(jnp.logical_not(turns))
-                def _():
-                    end(i, yb2).start()
+                hop2(i, KH).wait_recv()
+                end(i, yb2, KH).start()
 
     def forward_end(i):
         @pl.when((core == 0) & turns if i < LP else turn_peer)
@@ -346,8 +369,7 @@
     forward_end(4)
 
     load_partner.wait()
-    for copy in own_u():
-        copy.wait()
+    pltpu.make_async_copy(uo, uo, lo.at[0]).wait()
 
     def locate(b):
         q = b // FL
@@ -376,11 +398,10 @@
         acc[b, 0] = times(rows, u2a, index)
         acc[b, 1] = times(rows, u3a, index)
 
-    def rest(b):
+    def rest(b, j):
         f, q, index = locate(b)
-        rows = hr[b, NS - 1]
-        out[f, q, :, 2 * W:3 * W] = (acc[b, 0] + times(rows, u2b, index)).astype(jnp.bfloat16)
-        out[f, q, :, 3 * W:4 * W] = (acc[b, 1] + times(rows, u3b, index)).astype(jnp.bfloat16)
+        value = acc[b, j] + times(hr[b, NS - 1], (u2b, u3b)[j], index)
+        out[f, q, :, (2 + j) * W:(3 + j) * W] = value.astype(jnp.bfloat16)
 
     def early(b, _):
         arrive(b)
@@ -397,13 +418,21 @@
         part(b)
         return 0
 
-    def last(b, _):
-        rest(b)
-        return 0
+    def last(j):
+        def body(b, _):
+            rest(b, j)
+            return 0
+
+        lax.fori_loop(0, B, body, 0, unroll=True)
 
     follow0.wait_recv()
     follow1.wait_recv()
     lax.fori_loop(0, B - 2, early, 0)
+
+    @pl.when(head_peer)
+    def _():
+        lax.fori_loop(B - 2, B, early, 0)
+
     follow2a.wait_recv()
 
     @pl.when(core == 0)
@@ -412,29 +441,40 @@
 
     @pl.when(core == 1)
     def _():
-        for i in range(LP - 1):
-            end(i, yb2).wait_recv()
+        pieces = u3a.at[pl.ds(SD, SD)]
+        pltpu.make_async_copy(pieces, pieces, l3_r.at[0]).wait()
 
     lax.fori_loop(0, B - 2, middle, 0, unroll=True)
-    lax.fori_loop(B - 2, B, late, 0, unroll=True)
+
+    @pl.when(head_peer)
+    def _():
+        lax.fori_loop(B - 2, B, middle, 0, unroll=True)
 
     @pl.when(jnp.logical_not(head_peer))
     def _():
+        lax.fori_loop(B - 2, B, late, 0, unroll=True)
         follow2b.wait_recv()
+        last(0)
+
+    @pl.when(core == 0)
+    def _():
+        follow3b.wait_recv()
+
+    @pl.when((core == 1) & jnp.logical_not(spare_to))
+    def _():
+        end(LP - 1, yb2).wait_recv()
+
+    @pl.when(spare_to)
+    def _():
+        end(LP - 1, yb2, KH).wait_recv()
+        follow3c.wait_recv()
+
+    last(1)
 
     @pl.when(head_peer)
     def _():
         end(LP, yb2).wait_recv()
-
-    @pl.when((core == 0) | spare_to)
-    def _():
-        follow3b.wait_recv()
-
-    @pl.when((core == 1) & jnp.logical_not(spare_to))
-    def _():
-        end(LP - 1, yb2).wait_recv()
-
-    lax.fori_loop(0, B, last, 0, unroll=True)
+        last(0)
 
     def sent(ref, sem):
         pltpu.make_async_copy(ref, ref, sem.at[0]).wait()
@@ -450,7 +490,15 @@
         def _():
             sent(half.at[0], y_s)
 
-        @pl.when(head | turn_peer)
+        @pl.when(head)
+        def _():
+            sent(half.at[0, pl.ds(0, 3)], y_s)
+
+        @pl.when(passes)
+        def _():
+            sent(half.at[0, 0], y_s)
+
+        @pl.when(turn_peer)
         def _():
             sent(half.at[0, pl.ds(0, 2)], y_s)
 
@@ -495,9 +543,9 @@
             pltpu.VMEM((LP + 1, SD, KB, W), bf16),
             pltpu.VMEM((LP + 1, SD, KB, W), bf16),
             pltpu.VMEM((B, 2, W, W), jnp.float32),
-            dma((NS, SD)), dma((B,)), dma((6,)),
-            dma((1,)), dma((B,)), dma((B, 2)),
-            dma((1,)), dma((6,)), *[dma((LP + 1,)) for _ in range(3)], dma((1,)), dma((LP + 1,)), pltpu.SemaphoreType.REGULAR,
+            dma((NS + 1,)), dma((B,)), dma((1,)),
+            dma((1,)), dma((B,)), dma((B,)),
+            dma((1,)), dma((6,)), dma((LP + 1,)), dma((LP + 1,)), dma((3,)), dma((1,)), dma((LP + 1,)), pltpu.SemaphoreType.REGULAR,
             pltpu.SMEM((SD, FL), jnp.int32), dma((1,)),
         ],
         compiler_params=pltpu.CompilerParams(

time: 45.3 us -> 44.5 us (0.982)
  Pallas kernels: 43.3 us -> 42.7 us
    pallas_call x1, Pallas kernels: 43.3 us -> 42.7 us  [local(): pl.pallas_call(kernel, out_shape=pltpu.VMEM((FL, SD, W, NB), bf16), in_sp...]
where the time goes in v4:
time: 44.5 us; the launch traced here: 44.4 us
  Pallas kernels  42.7 us (96%)
  local copies, waits for them, and re-layouts  1.67 us (4%)
    pallas_call x1, Pallas kernels, local(): pl.pallas_call(kernel, out_shape=pltpu.VMEM((FL, SD, W, NB), bf16), in_sp...  42.7 us
    unnamed x1, local copies, waits for them, and re-layouts  1.67 us

profile of v4, /device:TPU:249, one launch (start us, length us, event | category | flops | bytes accessed | tf_op | source)
XLA Modules:
  0.0 44.4 jit_solution(8263615088789532255)
XLA Ops:
  0.0 42.7 %shard_map.37 = bf16[3,2,256,1024]{3,2,1,0:T(8,128)(2,1)S(1)} custom-call(bf16[2,1024,1024]{2,1,0:T(8,128)(2,1)} %basis.1, bf16[3,2,1024,256]{3,2,1,0:T(8,128)(2,1)} %fermion.1, s32[2,3]{1,0:T(2,128)} %bitcast.1), custom_call_target="tpu_custom_call" | custom-call | tf_op jit(solution)/shard_map/pallas_call | solution.py:521
  42.7 1.7 %copy.5 = bf16[3,2,256,1024]{3,2,1,0:T(8,128)(2,1)} copy(bf16[3,2,256,1024]{3,2,1,0:T(8,128)(2,1)S(1)} %shard_map.37) | data formatting | bytes 6291456

commit v5 on v4

--- a/solution.py
+++ b/solution.py
@@ -25,7 +25,7 @@
 def kernel(
     basis, fermion, partner_in, out,
     uo, u0, u1, u2a, u2b, u3a, u3b, fer, half, hr, rbuf, yb1, yb2, yb3, acc,
-    lu, lf, lo, x_s, x_r, r1_r, y_s, y_r, l1_r, l2_r, l3_r, t_s, t_r, answer, partner, p_s,
+    lu, lf, lo, x_s, x_r, r1_r, y_s, y_r, l1_r, l2_r, l3_r, t_s, t_r, answer, x_answer, partner, p_s,
 ):
     sec = lax.axis_index("sec")
     me = lax.axis_index("slab")
@@ -62,8 +62,13 @@
     def greet(device):
         pl.semaphore_signal(barrier, inc=1, device_id=device, device_id_type=MESH)
 
-    greet(right)
-    greet(left)
+    @pl.when(me != NS - 1)
+    def _():
+        greet(right)
+
+    @pl.when(me != 1)
+    def _():
+        greet(left)
 
     @pl.when(jnp.logical_not(head_peer))
     def _():
@@ -198,7 +203,15 @@
     greeted = jnp.where(
         core == 1, 3 + one(head_peer), 5 - one(head) + one(turns & (z != 0)) + one(turn_peer)
     )
-    pl.semaphore_wait(barrier, greeted)
+    pl.semaphore_wait(barrier, greeted - 2 * one(me == 0))
+
+    @pl.when(me == 1)
+    def _():
+        pl.semaphore_signal(x_answer, inc=1, device_id=left, device_id_type=MESH)
+
+    @pl.when(me == NS - 1)
+    def _():
+        pl.semaphore_signal(x_answer, inc=1, device_id=right, device_id_type=MESH)
 
     @pl.when(turn_peer)
     def _():
@@ -253,6 +266,11 @@
             uo[xo, 0, :, k * H:(k + 1) * H], fer[0], (((0,), (0,)), ((), ())),
             preferred_element_type=jnp.float32,
         ).astype(jnp.bfloat16)
+
+    @pl.when(me == 0)
+    def _():
+        pl.semaphore_wait(x_answer, 2)
+
     relay1(0, 0).start()
     load_uo(xp, 0).wait()
     half[0, xp] = first_product(0, 0, xp)
@@ -392,11 +410,9 @@
         out[f, q, :, 0:W] = times(rows, u0, index).astype(jnp.bfloat16)
         out[f, q, :, W:2 * W] = times(rows, u1, index).astype(jnp.bfloat16)
 
-    def part(b):
+    def part(b, j):
         f, q, index = locate(b)
-        rows = rows_of(b, 0, NS - 1)
-        acc[b, 0] = times(rows, u2a, index)
-        acc[b, 1] = times(rows, u3a, index)
+        acc[b, j] = times(rows_of(b, 0, NS - 1), (u2a, u3a)[j], index)
 
     def rest(b, j):
         f, q, index = locate(b)
@@ -409,14 +425,23 @@
         return 0
 
     def middle(b, _):
-        part(b)
+        part(b, 0)
+        part(b, 1)
         return 0
 
     def late(b, _):
         arrive(b)
         whole(b)
-        part(b)
+        part(b, 0)
+        part(b, 1)
         return 0
+
+    def parts(j):
+        def body(b, _):
+            part(b, j)
+            return 0
+
+        lax.fori_loop(0, B, body, 0, unroll=True)
 
     def last(j):
         def body(b, _):
@@ -429,29 +454,31 @@
     follow1.wait_recv()
     lax.fori_loop(0, B - 2, early, 0)
 
-    @pl.when(head_peer)
-    def _():
-        lax.fori_loop(B - 2, B, early, 0)
-
-    follow2a.wait_recv()
-
     @pl.when(core == 0)
     def _():
         follow3a.wait_recv()
 
-    @pl.when(core == 1)
-    def _():
+    def long_way():
         pieces = u3a.at[pl.ds(SD, SD)]
         pltpu.make_async_copy(pieces, pieces, l3_r.at[0]).wait()
 
-    lax.fori_loop(0, B - 2, middle, 0, unroll=True)
-
     @pl.when(head_peer)
     def _():
-        lax.fori_loop(B - 2, B, middle, 0, unroll=True)
+        lax.fori_loop(B - 2, B, early, 0)
+        long_way()
+        parts(1)
+        follow2a.wait_recv()
+        parts(0)
 
     @pl.when(jnp.logical_not(head_peer))
     def _():
+        follow2a.wait_recv()
+
+        @pl.when(core == 1)
+        def _():
+            long_way()
+
+        lax.fori_loop(0, B - 2, middle, 0, unroll=True)
         lax.fori_loop(B - 2, B, late, 0, unroll=True)
         follow2b.wait_recv()
         last(0)
@@ -545,7 +572,7 @@
             pltpu.VMEM((B, 2, W, W), jnp.float32),
             dma((NS + 1,)), dma((B,)), dma((1,)),
             dma((1,)), dma((B,)), dma((B,)),
-            dma((1,)), dma((6,)), dma((LP + 1,)), dma((LP + 1,)), dma((3,)), dma((1,)), dma((LP + 1,)), pltpu.SemaphoreType.REGULAR,
+            dma((1,)), dma((6,)), dma((LP + 1,)), dma((LP + 1,)), dma((3,)), dma((1,)), dma((LP + 1,)), pltpu.SemaphoreType.REGULAR, pltpu.SemaphoreType.REGULAR,
             pltpu.SMEM((SD, FL), jnp.int32), dma((1,)),
         ],
         compiler_params=pltpu.CompilerParams(

time: 44.5 us -> 43.8 us (0.984)
  Pallas kernels: 42.7 us -> 42 us
    pallas_call x1, Pallas kernels: 42.7 us -> 42 us  [local(): pl.pallas_call(kernel, out_shape=pltpu.VMEM((FL, SD, W, NB), bf16), in_sp...]
where the time goes in v5:
time: 43.8 us; the launch traced here: 43.7 us
  Pallas kernels  42 us (96%)
  local copies, waits for them, and re-layouts  1.67 us (4%)
    pallas_call x1, Pallas kernels, local(): pl.pallas_call(kernel, out_shape=pltpu.VMEM((FL, SD, W, NB), bf16), in_sp...  42 us
    unnamed x1, local copies, waits for them, and re-layouts  1.67 us

profile of v5, /device:TPU:249, one launch (start us, length us, event | category | flops | bytes accessed | tf_op | source)
XLA Modules:
  0.0 43.7 jit_solution(13058115155036090993)
XLA Ops:
  0.0 42.0 %shard_map.37 = bf16[3,2,256,1024]{3,2,1,0:T(8,128)(2,1)S(1)} custom-call(bf16[2,1024,1024]{2,1,0:T(8,128)(2,1)} %basis.1, bf16[3,2,1024,256]{3,2,1,0:T(8,128)(2,1)} %fermion.1, s32[2,3]{1,0:T(2,128)} %bitcast.1), custom_call_target="tpu_custom_call" | custom-call | tf_op jit(solution)/shard_map/pallas_call | solution.py:548
  42.0 1.7 %copy.5 = bf16[3,2,256,1024]{3,2,1,0:T(8,128)(2,1)} copy(bf16[3,2,256,1024]{3,2,1,0:T(8,128)(2,1)S(1)} %shard_map.37) | data formatting | bytes 6291456

commit v6 on v5

--- a/solution.py
+++ b/solution.py
@@ -255,12 +255,6 @@
     load_uo(xo, 0).wait()
     for j in (xm, me):
         load_uo(j, 0).start()
-    for j in (0, 3, 1, 2):
-        load_uo(j, 1).start()
-    for f in range(1, FL):
-        load_f(f, f, 0).start()
-    for f in range(FL):
-        load_f(FL + f, f, 1).start()
     for k in range(2):
         half[0, xo, k * H:(k + 1) * H] = lax.dot_general(
             uo[xo, 0, :, k * H:(k + 1) * H], fer[0], (((0,), (0,)), ((), ())),
@@ -272,6 +266,12 @@
         pl.semaphore_wait(x_answer, 2)
 
     relay1(0, 0).start()
+    for f in range(1, FL):
+        load_f(f, f, 0).start()
+    for j in range(NS):
+        load_uo(j, 1).start()
+    for f in range(FL):
+        load_f(FL + f, f, 1).start()
     load_uo(xp, 0).wait()
     half[0, xp] = first_product(0, 0, xp)
     relay1(0, 1).start()
@@ -297,14 +297,14 @@
         direct(b, 1).start()
         return 0
 
-    lax.fori_loop(1, 4, stage1, 0)
+    lax.fori_loop(1, 2, stage1, 0)
 
     @pl.when(head)
     def _():
         pl.semaphore_wait(answer, 1)
         send_chunks()
 
-    lax.fori_loop(4, B, stage1, 0)
+    lax.fori_loop(2, B, stage1, 0)
     for copy in own_u():
         copy.start()
 
@@ -424,11 +424,6 @@
         whole(b)
         return 0
 
-    def middle(b, _):
-        part(b, 0)
-        part(b, 1)
-        return 0
-
     def late(b, _):
         arrive(b)
         whole(b)
@@ -436,12 +431,22 @@
         part(b, 1)
         return 0
 
-    def parts(j):
+    def complete(b, _):
+        arrive(b)
+        whole(b)
+        f, q, index = locate(b)
+        most, rows = rows_of(b, 0, NS - 1), hr[b, NS - 1]
+        for j, (ua, ub) in enumerate(((u2a, u2b), (u3a, u3b))):
+            value = times(most, ua, index) + times(rows, ub, index)
+            out[f, q, :, (2 + j) * W:(3 + j) * W] = value.astype(jnp.bfloat16)
+        return 0
+
+    def parts(j, low, high):
         def body(b, _):
             part(b, j)
             return 0
 
-        lax.fori_loop(0, B, body, 0, unroll=True)
+        lax.fori_loop(low, high, body, 0, unroll=True)
 
     def last(j):
         def body(b, _):
@@ -450,58 +455,67 @@
 
         lax.fori_loop(0, B, body, 0, unroll=True)
 
-    follow0.wait_recv()
-    follow1.wait_recv()
-    lax.fori_loop(0, B - 2, early, 0)
-
-    @pl.when(core == 0)
-    def _():
-        follow3a.wait_recv()
-
     def long_way():
         pieces = u3a.at[pl.ds(SD, SD)]
         pltpu.make_async_copy(pieces, pieces, l3_r.at[0]).wait()
 
-    @pl.when(head_peer)
-    def _():
-        lax.fori_loop(B - 2, B, early, 0)
-        long_way()
-        parts(1)
-        follow2a.wait_recv()
-        parts(0)
-
-    @pl.when(jnp.logical_not(head_peer))
-    def _():
-        follow2a.wait_recv()
-
-        @pl.when(core == 1)
-        def _():
+    @pl.when(core == 0)
+    def _():
+        for copy in (follow0, follow1, follow2a, follow2b, follow3a, follow3b):
+            copy.wait_recv()
+        lax.fori_loop(0, B, complete, 0)
+
+    late_direct = head_peer | ((core == 1) & (y == NY - 1) & (z == nz // 2 - 1))
+
+    @pl.when(core == 1)
+    def _():
+        follow0.wait_recv()
+        follow1.wait_recv()
+        lax.fori_loop(0, B - 2, early, 0)
+
+        @pl.when(late_direct)
+        def _():
+            early(B - 2, 0)
             long_way()
-
-        lax.fori_loop(0, B - 2, middle, 0, unroll=True)
-        lax.fori_loop(B - 2, B, late, 0, unroll=True)
-        follow2b.wait_recv()
-        last(0)
-
-    @pl.when(core == 0)
-    def _():
-        follow3b.wait_recv()
-
-    @pl.when((core == 1) & jnp.logical_not(spare_to))
-    def _():
-        end(LP - 1, yb2).wait_recv()
-
-    @pl.when(spare_to)
-    def _():
-        end(LP - 1, yb2, KH).wait_recv()
-        follow3c.wait_recv()
-
-    last(1)
-
-    @pl.when(head_peer)
-    def _():
-        end(LP, yb2).wait_recv()
-        last(0)
+            parts(1, 0, B - 1)
+            follow2a.wait_recv()
+            parts(0, 0, B - 1)
+            late(B - 1, 0)
+
+        @pl.when(jnp.logical_not(late_direct))
+        def _():
+            follow2a.wait_recv()
+            parts(0, 0, B - 2)
+            early(B - 2, 0)
+            part(B - 2, 0)
+            long_way()
+            parts(1, 0, B - 1)
+            late(B - 1, 0)
+            follow2b.wait_recv()
+            last(0)
+
+        @pl.when(jnp.logical_not(spare_to))
+        def _():
+            end(LP - 1, yb2).wait_recv()
+
+        @pl.when(spare_to)
+        def _():
+            end(LP - 1, yb2, KH).wait_recv()
+            follow3c.wait_recv()
+
+        last(1)
+
+        @pl.when(late_direct)
+        def _():
+            @pl.when(head_peer)
+            def _():
+                end(LP, yb2).wait_recv()
+
+            @pl.when(jnp.logical_not(head_peer))
+            def _():
+                follow2b.wait_recv()
+
+            last(0)
 
     def sent(ref, sem):
         pltpu.make_async_copy(ref, ref, sem.at[0]).wait()

time: 43.8 us -> 43.5 us (level)
    pallas_call x1, Pallas kernels: 42 us -> 41.6 us  [local(): pl.pallas_call(kernel, out_shape=pltpu.VMEM((FL, SD, W, NB), bf16), in_sp...]
where the time goes in v6:
time: 43.5 us; the launch traced here: 43.2 us
  Pallas kernels  41.6 us (96%)
  local copies, waits for them, and re-layouts  1.67 us (4%)
    pallas_call x1, Pallas kernels, local(): pl.pallas_call(kernel, out_shape=pltpu.VMEM((FL, SD, W, NB), bf16), in_sp...  41.6 us
    unnamed x1, local copies, waits for them, and re-layouts  1.67 us

profile of v6, /device:TPU:249, one launch (start us, length us, event | category | flops | bytes accessed | tf_op | source)
XLA Modules:
  0.0 43.2 jit_solution(17529172545992471304)
XLA Ops:
  0.0 41.6 %shard_map.37 = bf16[3,2,256,1024]{3,2,1,0:T(8,128)(2,1)S(1)} custom-call(bf16[2,1024,1024]{2,1,0:T(8,128)(2,1)} %basis.1, bf16[3,2,1024,256]{3,2,1,0:T(8,128)(2,1)} %fermion.1, s32[2,3]{1,0:T(2,128)} %bitcast.1), custom_call_target="tpu_custom_call" | custom-call | tf_op jit(solution)/shard_map/pallas_call | solution.py:562
  41.6 1.7 %copy.5 = bf16[3,2,256,1024]{3,2,1,0:T(8,128)(2,1)} copy(bf16[3,2,256,1024]{3,2,1,0:T(8,128)(2,1)S(1)} %shard_map.37) | data formatting | bytes 6291456

commit v7 on v6

--- a/solution.py
+++ b/solution.py
@@ -62,11 +62,11 @@
     def greet(device):
         pl.semaphore_signal(barrier, inc=1, device_id=device, device_id_type=MESH)
 
-    @pl.when(me != NS - 1)
+    @pl.when(me < NS // 2)
     def _():
         greet(right)
 
-    @pl.when(me != 1)
+    @pl.when((me == 0) | (me == NS - 1))
     def _():
         greet(left)
 
@@ -203,13 +203,13 @@
     greeted = jnp.where(
         core == 1, 3 + one(head_peer), 5 - one(head) + one(turns & (z != 0)) + one(turn_peer)
     )
-    pl.semaphore_wait(barrier, greeted - 2 * one(me == 0))
-
-    @pl.when(me == 1)
+    pl.semaphore_wait(barrier, greeted - 2 * one(me == 0) - one((me == 1) | (me == NS - 1)))
+
+    @pl.when((me == 1) | (me == NS // 2))
     def _():
         pl.semaphore_signal(x_answer, inc=1, device_id=left, device_id_type=MESH)
 
-    @pl.when(me == NS - 1)
+    @pl.when(me >= NS // 2)
     def _():
         pl.semaphore_signal(x_answer, inc=1, device_id=right, device_id_type=MESH)
 
@@ -264,6 +264,10 @@
     @pl.when(me == 0)
     def _():
         pl.semaphore_wait(x_answer, 2)
+
+    @pl.when((me == 1) | (me == NS - 1))
+    def _():
+        pl.semaphore_wait(x_answer, 1)
 
     relay1(0, 0).start()
     for f in range(1, FL):

time: 43.5 us -> 43.3 us (level)
  no operation moved by 1% of the time
where the time goes in v7:
time: 43.3 us; the launch traced here: 43.2 us
  Pallas kernels  41.6 us (96%)
  local copies, waits for them, and re-layouts  1.67 us (4%)
    pallas_call x1, Pallas kernels, local(): pl.pallas_call(kernel, out_shape=pltpu.VMEM((FL, SD, W, NB), bf16), in_sp...  41.6 us
    unnamed x1, local copies, waits for them, and re-layouts  1.67 us

profile of v7, /device:TPU:249, one launch (start us, length us, event | category | flops | bytes accessed | tf_op | source)
XLA Modules:
  0.0 43.2 jit_solution(16016384509212170702)
XLA Ops:
  0.0 41.6 %shard_map.37 = bf16[3,2,256,1024]{3,2,1,0:T(8,128)(2,1)S(1)} custom-call(bf16[2,1024,1024]{2,1,0:T(8,128)(2,1)} %basis.1, bf16[3,2,1024,256]{3,2,1,0:T(8,128)(2,1)} %fermion.1, s32[2,3]{1,0:T(2,128)} %bitcast.1), custom_call_target="tpu_custom_call" | custom-call | tf_op jit(solution)/shard_map/pallas_call | solution.py:566
  41.6 1.7 %copy.5 = bf16[3,2,256,1024]{3,2,1,0:T(8,128)(2,1)} copy(bf16[3,2,256,1024]{3,2,1,0:T(8,128)(2,1)S(1)} %shard_map.37) | data formatting | bytes 6291456

commit v8 on v7

--- a/solution.py
+++ b/solution.py
@@ -25,7 +25,7 @@
 def kernel(
     basis, fermion, partner_in, out,
     uo, u0, u1, u2a, u2b, u3a, u3b, fer, half, hr, rbuf, yb1, yb2, yb3, acc,
-    lu, lf, lo, x_s, x_r, r1_r, y_s, y_r, l1_r, l2_r, l3_r, t_s, t_r, answer, x_answer, partner, p_s,
+    lu, lf, lo, sent_s, x_r, r1_r, y_r, l1_r, l2_r, l3_r, t_r, answer, x_answer, partner, p_s,
 ):
     sec = lax.axis_index("sec")
     me = lax.axis_index("slab")
@@ -100,7 +100,7 @@
         )
 
     def load_f(b, f, q):
-        return pltpu.make_async_copy(fermion.at[f, q], fer.at[b], lf.at[b])
+        return pltpu.make_async_copy(fermion.at[f, q], fer.at[b], lf.at[min(b, 1)])
 
     def load_u(ref, j, row, rows):
         return pltpu.make_async_copy(
@@ -121,11 +121,11 @@
     def follow(src, dst, n):
         return pltpu.make_async_remote_copy(
             src_ref=src, dst_ref=dst.at[pl.ds(SD, SD)],
-            send_sem=y_s.at[0], recv_sem=y_r.at[n], device_id=before, device_id_type=MESH,
+            send_sem=sent_s.at[0], recv_sem=y_r.at[n], device_id=before, device_id_type=MESH,
         )
 
     follow0 = follow(basis.at[:, :, pl.ds(0, W)], u0, 0)
-    follow1 = follow(basis.at[:, :, pl.ds(W, W)], u1, 1)
+    follow1 = follow(basis.at[:, :, pl.ds(W, W)], u1, 0)
     follow2a = follow(basis.at[:, pl.ds(0, KA), pl.ds(2 * W, W)], u2a, 2)
     follow2b = follow(basis.at[:, pl.ds(KA, KB), pl.ds(2 * W, W)], u2b, 3)
     follow3a = follow(basis.at[:, pl.ds(0, KA), pl.ds(3 * W, W)], u3a, 4)
@@ -134,7 +134,7 @@
     follow3c = pltpu.make_async_remote_copy(
         src_ref=basis.at[:, pl.ds(KA + KH, KH), pl.ds(3 * W, W)],
         dst_ref=u3b.at[pl.ds(SD, SD), pl.ds(KH, KH)],
-        send_sem=y_s.at[0], recv_sem=y_r.at[5], device_id=before, device_id_type=MESH,
+        send_sem=sent_s.at[0], recv_sem=y_r.at[5], device_id=before, device_id_type=MESH,
     )
 
     def hop1(i, rows=KB):
@@ -144,19 +144,19 @@
             source = basis.at[:, pl.ds(KA, KB), pl.ds(2 * W, W)]
         return pltpu.make_async_remote_copy(
             src_ref=source, dst_ref=yb1.at[i, :, pl.ds(0, rows)],
-            send_sem=y_s.at[0], recv_sem=l1_r.at[i], device_id=hop_to, device_id_type=MESH,
+            send_sem=sent_s.at[0], recv_sem=l1_r.at[i], device_id=hop_to, device_id_type=MESH,
         )
 
     def hop2(i, rows=KB):
         return pltpu.make_async_remote_copy(
             src_ref=yb1.at[i, :, pl.ds(0, rows)], dst_ref=yb2.at[i, :, pl.ds(0, rows)],
-            send_sem=y_s.at[0], recv_sem=l2_r.at[i], device_id=hop_to, device_id_type=MESH,
+            send_sem=sent_s.at[0], recv_sem=l2_r.at[i], device_id=hop_to, device_id_type=MESH,
         )
 
     def turn(i):
         return pltpu.make_async_remote_copy(
             src_ref=yb2.at[i], dst_ref=yb3.at[i],
-            send_sem=t_s.at[0], recv_sem=t_r.at[i], device_id=row_to, device_id_type=MESH,
+            send_sem=sent_s.at[0], recv_sem=t_r.at[i], device_id=row_to, device_id_type=MESH,
         )
 
     def end(i, src, rows=KB):
@@ -166,7 +166,7 @@
             target = (u3b if i == LP - 1 else u2b).at[pl.ds(SD, SD), pl.ds(0, rows)]
         return pltpu.make_async_remote_copy(
             src_ref=src.at[i, :, pl.ds(0, rows)], dst_ref=target,
-            send_sem=y_s.at[0], recv_sem=l3_r.at[max(0, i - LP + 2)], device_id=end_to, device_id_type=MESH,
+            send_sem=sent_s.at[0], recv_sem=l3_r.at[max(0, i - LP + 2)], device_id=end_to, device_id_type=MESH,
         )
 
     H = W // 2
@@ -174,21 +174,21 @@
     def direct(b, k):
         return pltpu.make_async_remote_copy(
             src_ref=half.at[b, (xp, xm)[k]], dst_ref=hr.at[b, me],
-            send_sem=x_s.at[0], recv_sem=x_r.at[b],
+            send_sem=sent_s.at[0], recv_sem=x_r.at[b],
             device_id=(right, left)[k], device_id_type=MESH,
         )
 
     def relay1(b, k):
         return pltpu.make_async_remote_copy(
             src_ref=half.at[b, xo, pl.ds(k * H, H)], dst_ref=rbuf.at[b, k],
-            send_sem=x_s.at[0], recv_sem=r1_r.at[b],
+            send_sem=sent_s.at[0], recv_sem=r1_r.at[b],
             device_id=(right, left)[k], device_id_type=MESH,
         )
 
     def relay2(b, k):
         return pltpu.make_async_remote_copy(
             src_ref=rbuf.at[b, k], dst_ref=hr.at[b, (xm, xp)[k], pl.ds(k * H, H)],
-            send_sem=x_s.at[0], recv_sem=x_r.at[b],
+            send_sem=sent_s.at[0], recv_sem=x_r.at[b],
             device_id=(right, left)[k], device_id_type=MESH,
         )
 
@@ -288,9 +288,11 @@
     second = uo.at[:, 1]
     pltpu.make_async_copy(second, second, lu.at[NS]).wait()
 
+    others = fer.at[pl.ds(1, B - 1)]
+    pltpu.make_async_copy(others, others, lf.at[1]).wait()
+
     def stage1(b, _):
         q = b // FL
-        load_f(b, 0, 0).wait()
         half[b, xo] = first_product(b, q, xo)
         half[b, xp] = first_product(b, q, xp)
         relay1(b, 0).start()
@@ -463,9 +465,13 @@
         pieces = u3a.at[pl.ds(SD, SD)]
         pltpu.make_async_copy(pieces, pieces, l3_r.at[0]).wait()
 
+    def first_chunks():
+        pltpu.make_async_copy(u0, u0, y_r.at[0]).wait()
+
     @pl.when(core == 0)
     def _():
-        for copy in (follow0, follow1, follow2a, follow2b, follow3a, follow3b):
+        first_chunks()
+        for copy in (follow2a, follow2b, follow3a, follow3b):
             copy.wait_recv()
         lax.fori_loop(0, B, complete, 0)
 
@@ -473,8 +479,7 @@
 
     @pl.when(core == 1)
     def _():
-        follow0.wait_recv()
-        follow1.wait_recv()
+        first_chunks()
         lax.fori_loop(0, B - 2, early, 0)
 
         @pl.when(late_direct)
@@ -521,43 +526,43 @@
 
             last(0)
 
-    def sent(ref, sem):
-        pltpu.make_async_copy(ref, ref, sem.at[0]).wait()
-
-    sent(hr, x_s)
+    def sent(ref):
+        pltpu.make_async_copy(ref, ref, sent_s.at[0]).wait()
+
+    sent(hr)
 
     @pl.when(core == 0)
     def _():
-        sent(fer, y_s)
-        sent(half.at[pl.ds(0, B - 1)], y_s)
+        sent(fer)
+        sent(half.at[pl.ds(0, B - 1)])
 
         @pl.when(jnp.logical_not(head))
         def _():
-            sent(half.at[0], y_s)
+            sent(half.at[0])
 
         @pl.when(head)
         def _():
-            sent(half.at[0, pl.ds(0, 3)], y_s)
+            sent(half.at[0, pl.ds(0, 3)])
 
         @pl.when(passes)
         def _():
-            sent(half.at[0, 0], y_s)
+            sent(half.at[0, 0])
 
         @pl.when(turn_peer)
         def _():
-            sent(half.at[0, pl.ds(0, 2)], y_s)
+            sent(half.at[0, pl.ds(0, 2)])
 
         @pl.when(turns)
         def _():
-            sent(yb2.at[pl.ds(0, LP)], t_s)
+            sent(yb2.at[pl.ds(0, LP)])
 
         @pl.when(turn_head)
         def _():
-            sent(yb2.at[LP], t_s)
+            sent(yb2.at[LP])
 
     @pl.when(core == 1)
     def _():
-        sent(uo, y_s)
+        sent(uo)
 
 
 def local(basis, fermion, partner):
@@ -588,9 +593,10 @@
             pltpu.VMEM((LP + 1, SD, KB, W), bf16),
             pltpu.VMEM((LP + 1, SD, KB, W), bf16),
             pltpu.VMEM((B, 2, W, W), jnp.float32),
-            dma((NS + 1,)), dma((B,)), dma((1,)),
+            dma((NS + 1,)), dma((2,)), dma((1,)),
             dma((1,)), dma((B,)), dma((B,)),
-            dma((1,)), dma((6,)), dma((LP + 1,)), dma((LP + 1,)), dma((3,)), dma((1,)), dma((LP + 1,)), pltpu.SemaphoreType.REGULAR, pltpu.SemaphoreType.REGULAR,
+            dma((6,)), dma((LP + 1,)), dma((LP + 1,)), dma((3,)), dma((LP + 1,)),
+            pltpu.SemaphoreType.REGULAR, pltpu.SemaphoreType.REGULAR,
             pltpu.SMEM((SD, FL), jnp.int32), dma((1,)),
         ],
         compiler_params=pltpu.CompilerParams(

time: 43.3 us -> 43.5 us (level)
  no operation moved by 1% of the time
where the time goes in v8:
time: 43.5 us; the launch traced here: 43.4 us
  Pallas kernels  41.7 us (96%)
  local copies, waits for them, and re-layouts  1.67 us (4%)
    pallas_call x1, Pallas kernels, local(): pl.pallas_call(kernel, out_shape=pltpu.VMEM((FL, SD, W, NB), bf16), in_sp...  41.7 us
    unnamed x1, local copies, waits for them, and re-layouts  1.67 us

profile of v8, /device:TPU:249, one launch (start us, length us, event | category | flops | bytes accessed | tf_op | source)
XLA Modules:
  0.0 43.4 jit_solution(6991121843279706874)
XLA Ops:
  0.0 41.7 %shard_map.37 = bf16[3,2,256,1024]{3,2,1,0:T(8,128)(2,1)S(1)} custom-call(bf16[2,1024,1024]{2,1,0:T(8,128)(2,1)} %basis.1, bf16[3,2,1024,256]{3,2,1,0:T(8,128)(2,1)} %fermion.1, s32[2,3]{1,0:T(2,128)} %bitcast.1), custom_call_target="tpu_custom_call" | custom-call | tf_op jit(solution)/shard_map/pallas_call | solution.py:571
  41.7 1.7 %copy.5 = bf16[3,2,256,1024]{3,2,1,0:T(8,128)(2,1)} copy(bf16[3,2,256,1024]{3,2,1,0:T(8,128)(2,1)S(1)} %shard_map.37) | data formatting | bytes 6291456

commit v9 on v7

--- a/solution.py
+++ b/solution.py
@@ -225,6 +225,23 @@
         for copy in (follow0, follow1, follow2a):
             copy.start()
 
+    @pl.when(core == 0)
+    def _():
+        for i in range(LP - 1):
+            hop1(i).start()
+
+    @pl.when((core == 0) & jnp.logical_not(spare))
+    def _():
+        hop1(LP - 1).start()
+
+    @pl.when(spare)
+    def _():
+        hop1(LP - 1, KH).start()
+
+    @pl.when(head)
+    def _():
+        hop1(LP).start()
+
     @pl.when((core == 0) & jnp.logical_not(head))
     def _():
         send_chunks()
@@ -233,23 +250,6 @@
     @pl.when(spare)
     def _():
         follow3c.start()
-
-    @pl.when(core == 0)
-    def _():
-        for i in range(LP - 1):
-            hop1(i).start()
-
-    @pl.when((core == 0) & jnp.logical_not(spare))
-    def _():
-        hop1(LP - 1).start()
-
-    @pl.when(spare)
-    def _():
-        hop1(LP - 1, KH).start()
-
-    @pl.when(head)
-    def _():
-        hop1(LP).start()
 
     load_f(0, 0, 0).wait()
     load_uo(xo, 0).wait()

time: 43.3 us -> 43.3 us (level)
  no operation moved by 1% of the time
where the time goes in v9:
time: 43.3 us; the launch traced here: 43.2 us
  Pallas kernels  41.6 us (96%)
  local copies, waits for them, and re-layouts  1.67 us (4%)
    pallas_call x1, Pallas kernels, local(): pl.pallas_call(kernel, out_shape=pltpu.VMEM((FL, SD, W, NB), bf16), in_sp...  41.6 us
    unnamed x1, local copies, waits for them, and re-layouts  1.67 us

profile of v9, /device:TPU:249, one launch (start us, length us, event | category | flops | bytes accessed | tf_op | source)
XLA Modules:
  0.0 43.2 jit_solution(14804588222677146887)
XLA Ops:
  0.0 41.6 %shard_map.37 = bf16[3,2,256,1024]{3,2,1,0:T(8,128)(2,1)S(1)} custom-call(bf16[2,1024,1024]{2,1,0:T(8,128)(2,1)} %basis.1, bf16[3,2,1024,256]{3,2,1,0:T(8,128)(2,1)} %fermion.1, s32[2,3]{1,0:T(2,128)} %bitcast.1), custom_call_target="tpu_custom_call" | custom-call | tf_op jit(solution)/shard_map/pallas_call | solution.py:566
  41.6 1.7 %copy.5 = bf16[3,2,256,1024]{3,2,1,0:T(8,128)(2,1)} copy(bf16[3,2,256,1024]{3,2,1,0:T(8,128)(2,1)S(1)} %shard_map.37) | data formatting | bytes 6291456
